TPU v7x, 32 devices: a whole 2x2x4 slice. The times are simulated.
32 devices in a mesh: ctx: 8 (over z, y), head: 4 (over x, core).
Axes of the slice: x: 2, y: 2, z: 4, core: 2. Of those that a mesh axis runs over, the one named last changes fastest.
Arguments:
- query_rows: bfloat16 [4096, 4096], P('ctx', 'head'), may hold values from -7.5 to 7.5
- key_rows: bfloat16 [4096, 4096], P('ctx', 'head'), may hold values from -7.5 to 7.5
- value_rows: bfloat16 [4096, 4096], P('ctx', 'head'), may hold values from -10 to 10
- centroids: float32 [32, 256, 128], P('head', 'ctx'), may hold values from -7.5 to 7.5
- norm_gain: float32 [4096], P('head'), may hold values from 0.1 to 1.9
- cluster_lists: int32 [32, 256, 32], P('head', 'ctx'), may hold values from 0 to 4095, as said below
- live_counts: int32 [32, 256, 8], P('head', 'ctx'), may hold values from 0 to 4, as said below
Outputs:
- normalized: bfloat16 [4096, 4096], P('ctx', 'head')
- swept_centroids: float32 [32, 256, 128], P('head', 'ctx')
- potentials: float32 [32, 256], P('head', 'ctx')
Inputs may be any that keep to these rules, and one draw needn't show every extreme that they name: `cluster_lists`: for each head every token appears in exactly one live slot. Slots k * 4 to (k+1) * 4 - 1 of a list form segment k; its first live_counts[h, c, k] slots hold, in rising order, tokens of k * 512 to (k+1) * 512 - 1; the other slots hold 0. `live_counts`: for each head, each k and each g, the counts of clusters g * 32 to (g+1) * 32 - 1 in segment k sum to exactly 64. In every head some cluster has all its segments full.
All inputs are finite; a program needn't handle non-finite values.
Results may differ from a plain program's by a relative error of at most 0.012.
Values may be sent and summed in bfloat16 or wider, within the bound.
No kernel may reach another device: no remote copies, remote signals or barrier semaphores. Data moves between devices by JAX's collectives and lax.ppermute only.
A program may use at most 64 MiB of HBM per device.

v0:
```python
import functools
import math

import jax
import jax.numpy as jnp
from jax import lax
from jax.experimental import pallas as pl
from jax.experimental.pallas import tpu as pltpu
from jax.sharding import PartitionSpec as P

ITERS = 5
LOG2E = math.log2(math.e)
TILE = 16
DIGIT = 64
LANES = 128
SMALLEST_MASS = 2.0**-80
VMEM = pl.BlockSpec(memory_space=pltpu.VMEM)
SMEM = pl.BlockSpec(memory_space=pltpu.SMEM)
BY_ROWS = (((1,), (1,)), ((), ()))


def block_attention(block_item):
    block_rows, positions, is_live = block_item
    head_dim = block_rows.shape[1] // 3
    query_part = block_rows[:, :head_dim]
    key_part = block_rows[:, head_dim : 2 * head_dim]
    value_part = block_rows[:, 2 * head_dim :]
    scores = lax.dot_general(
        query_part, key_part, (((1,), (1,)), ((), ())), preferred_element_type=jnp.float32
    ) * head_dim ** (-0.5)
    allowed = is_live[None, :] & (positions[None, :] <= positions[:, None])
    scores = jnp.where(allowed, scores, -1e30)
    peak_row = jnp.max(scores, axis=-1, keepdims=True)
    unnormed = jnp.exp(scores - peak_row)
    row_total = jnp.sum(unnormed, axis=-1, keepdims=True)
    blended = jnp.dot(unnormed.astype(jnp.bfloat16), value_part, preferred_element_type=jnp.float32)
    return (blended / row_total).astype(jnp.bfloat16)


def attend_blocks(block_rows, cluster_lists, owned_live):
    count_blocks = block_rows.shape[0]
    positions = cluster_lists.reshape(count_blocks, -1)
    is_live = owned_live.reshape(count_blocks, -1)
    return lax.map(block_attention, (block_rows, positions, is_live))


def balancing_sweeps(per_head_keys, centroids, device_index, context_length):
    head_dev, cluster_dev, head_dim = centroids.shape
    clusters = cluster_dev * context_length
    tok_dev = per_head_keys.shape[0]
    balance = math.log(tok_dev * context_length / clusters)
    rounded = lax.all_gather(centroids.astype(jnp.bfloat16), "ctx", axis=1, tiled=True)
    potential = jnp.zeros((head_dev, clusters), jnp.float32)
    current_mine = centroids
    for _ in range(ITERS):
        logits = (
            jnp.einsum("thd,hcd->thc", per_head_keys, rounded, preferred_element_type=jnp.float32)
            * head_dim ** (-0.5)
            + potential[None]
        )
        row_peak = jnp.max(logits, axis=-1, keepdims=True)
        log_total = row_peak + jnp.log(jnp.sum(jnp.exp(logits - row_peak), axis=-1, keepdims=True))
        logprob = logits - log_total
        column_peak = lax.pmax(jnp.max(logprob, axis=0), "ctx")
        weights = jnp.exp(logprob - column_peak[None])
        local_mass = jnp.sum(weights, axis=0)
        local_numerator = jnp.einsum(
            "thc,thd->hcd",
            weights.astype(jnp.bfloat16),
            per_head_keys,
            preferred_element_type=jnp.float32,
        )
        mass_total, numerator = lax.psum((local_mass, local_numerator), "ctx")
        current = numerator / mass_total[:, :, None]
        rounded = current.astype(jnp.bfloat16)
        current_mine = lax.dynamic_slice_in_dim(current, device_index * cluster_dev, cluster_dev, 1)
        potential = potential + balance - (column_peak + jnp.log(mass_total))
    return (
        current_mine,
        lax.dynamic_slice_in_dim(potential, device_index * cluster_dev, cluster_dev, 1),
    )


def local_wide(query_rows, key_rows, value_rows, centroids, norm_gain, cluster_lists, live_counts):
    context_length = lax.axis_size("ctx")
    device_index = lax.axis_index("ctx")
    tok_dev = query_rows.shape[0]
    head_dev, cluster_dev, head_dim = centroids.shape
    segment = cluster_lists.shape[2] // context_length
    query_heads = query_rows.reshape(tok_dev, head_dev, head_dim)
    per_head_keys = key_rows.reshape(tok_dev, head_dev, head_dim)
    value_heads = value_rows.reshape(tok_dev, head_dev, head_dim)
    swept_centroids, potentials = balancing_sweeps(
        per_head_keys, centroids, device_index, context_length
    )
    lists_split = cluster_lists.reshape(head_dev, cluster_dev, context_length, segment)
    asked_ids, asked_counts = (
        lax.all_to_all(lists_split, "ctx", split_axis=2, concat_axis=2, tiled=True),
        lax.all_to_all(live_counts, "ctx", split_axis=2, concat_axis=2, tiled=True),
    )
    slot_ids = jnp.arange(segment, dtype=jnp.int32)
    asked_live = slot_ids < asked_counts[..., None]
    local_ids = jnp.where(asked_live, asked_ids - device_index * tok_dev, 0)
    head_ids = jnp.broadcast_to(
        jnp.arange(head_dev, dtype=jnp.int32)[:, None, None, None], local_ids.shape
    )
    owned_live = slot_ids < live_counts[..., None]
    empty_out = jnp.zeros((tok_dev, head_dev, head_dim), jnp.bfloat16)
    sent_rows = jnp.concatenate(
        [
            query_heads[local_ids, head_ids],
            per_head_keys[local_ids, head_ids],
            value_heads[local_ids, head_ids],
        ],
        axis=-1,
    )
    arrived = lax.all_to_all(sent_rows, "ctx", split_axis=2, concat_axis=2, tiled=True)
    block_rows = arrived.reshape(head_dev * cluster_dev, context_length * segment, 3 * head_dim)
    block_out = attend_blocks(block_rows, cluster_lists, owned_live)
    returned = lax.all_to_all(
        block_out.reshape(head_dev, cluster_dev, context_length, segment, head_dim),
        "ctx",
        split_axis=2,
        concat_axis=2,
        tiled=True,
    )
    target = jnp.where(asked_live, local_ids, tok_dev)
    attended = empty_out.at[target, head_ids].set(returned, mode="drop")
    wide_attended = attended.reshape(tok_dev, head_dev * head_dim).astype(jnp.float32)
    squares = lax.psum(jnp.sum(wide_attended * wide_attended, axis=-1), "head")
    width = head_dev * head_dim * lax.axis_size("head")
    normalized = (wide_attended * lax.rsqrt(squares / width + 1e-06)[:, None] * norm_gain).astype(
        jnp.bfloat16
    )
    return (normalized, swept_centroids, potentials)


def dot(a, b):
    return jnp.dot(a, b, preferred_element_type=jnp.float32)


def sweeps_kernel(tok_dev, cluster_dev, *refs):
    sources = (len(refs) - 4) // 2
    blocks, outs = refs[:sources], refs[sources : 2 * sources]
    keys, current, potential, scaled = refs[-4:]
    tokens, head_dim = keys.shape
    clusters = sources * cluster_dev
    scale = head_dim**-0.5 * LOG2E
    balance = math.log2(tokens / clusters)
    tile, wide = 2 * tok_dev, min(4, sources) * tok_dev
    for s, block in enumerate(blocks):
        keys[s * tok_dev : (s + 1) * tok_dev, :] = block[:tok_dev, :]
        current[s * cluster_dev : (s + 1) * cluster_dev, :] = block[
            tok_dev : tok_dev + cluster_dev, :
        ].astype(jnp.float32)
    potential[...] = jnp.zeros_like(potential)

    def part(t, size):
        return pl.ds(pl.multiple_of(t * size, size), size)

    def logits_of(t, rounded, pot):
        return (
            lax.dot_general(
                rounded, keys[part(t, tile), :], BY_ROWS, preferred_element_type=jnp.float32
            )
            * scale
            + pot
        )

    def fold(total, values, op):
        for p in range(values.shape[1] // LANES):
            total = op(total, values[:, p * LANES : (p + 1) * LANES])
        return total

    def sweep(_, carry):
        rounded = current[...].astype(jnp.bfloat16)
        pot = potential[...]
        flat = jnp.zeros((clusters, LANES), jnp.float32)

        def members(t, peak):
            logits = logits_of(t, rounded, pot)
            shifted = jnp.exp2(logits - jnp.max(logits, axis=0, keepdims=True))
            member = shifted * (1.0 / jnp.sum(shifted, axis=0, keepdims=True))
            scaled[:, part(t, tile)] = member
            return fold(peak, member, jnp.maximum)

        peak = jnp.max(
            lax.fori_loop(0, tokens // tile, members, flat), axis=1, keepdims=True
        )
        inverse = 1.0 / jnp.maximum(peak, SMALLEST_MASS)

        def add(t, sums):
            numerator, mass = sums
            weights = scaled[:, part(t, wide)] * inverse
            numerator += dot(weights.astype(jnp.bfloat16), keys[part(t, wide), :])
            return numerator, fold(mass, weights, jnp.add)

        sums = (jnp.zeros((clusters, head_dim), jnp.float32), flat)
        numerator, mass = lax.fori_loop(0, tokens // wide, add, sums)
        mass_total = jnp.sum(mass, axis=1, keepdims=True)
        current[...] = numerator / mass_total
        potential[...] = pot + balance - (jnp.log2(peak) + jnp.log2(mass_total))

        @pl.when(jnp.min(peak) < SMALLEST_MASS)
        def _():
            def peaks(t, top):
                logits = logits_of(t, rounded, pot)
                row_peak = jnp.max(logits, axis=0, keepdims=True)
                total = jnp.sum(jnp.exp2(logits - row_peak), axis=0, keepdims=True)
                logprob = logits - (row_peak + jnp.log2(total))
                scaled[:, part(t, tile)] = logprob
                return jnp.maximum(top, jnp.max(logprob, axis=1, keepdims=True))

            lowest = jnp.full((clusters, 1), -jnp.inf, jnp.float32)
            top = lax.fori_loop(0, tokens // tile, peaks, lowest)

            def again(t, sums):
                numerator, mass = sums
                weights = jnp.exp2(scaled[:, part(t, wide)] - top)
                numerator += dot(weights.astype(jnp.bfloat16), keys[part(t, wide), :])
                return numerator, mass + jnp.sum(weights, axis=1, keepdims=True)

            zeros = (jnp.zeros((clusters, head_dim), jnp.float32), jnp.zeros_like(lowest))
            numerator, mass_total = lax.fori_loop(0, tokens // wide, again, zeros)
            current[...] = numerator / mass_total
            potential[...] = pot + balance - (top + jnp.log2(mass_total))

        return carry

    lax.fori_loop(0, ITERS, sweep, 0)
    shape = (cluster_dev, LANES)
    diagonal = lax.broadcasted_iota(jnp.int32, shape, 0) == lax.broadcasted_iota(
        jnp.int32, shape, 1
    )
    for s in range(sources):
        rows = slice(s * cluster_dev, (s + 1) * cluster_dev)
        outs[s][:cluster_dev, :] = current[rows, :]
        column = jnp.broadcast_to(potential[rows, :] * (1.0 / LOG2E), shape)
        line = jnp.sum(jnp.where(diagonal, column, 0.0), axis=0, keepdims=True)
        outs[s][cluster_dev:, :] = jnp.broadcast_to(line, (8, LANES))


def run_sweeps(blocks, tok_dev, cluster_dev):
    sources, head_dim = len(blocks), blocks[0].shape[1]
    tokens, clusters = sources * tok_dev, sources * cluster_dev
    return pl.pallas_call(
        functools.partial(sweeps_kernel, tok_dev, cluster_dev),
        out_shape=[jax.ShapeDtypeStruct((cluster_dev + 8, head_dim), jnp.float32)] * sources,
        in_specs=[VMEM] * sources,
        out_specs=[VMEM] * sources,
        scratch_shapes=[
            pltpu.VMEM((tokens, head_dim), jnp.bfloat16),
            pltpu.VMEM((clusters, head_dim), jnp.float32),
            pltpu.VMEM((clusters, 1), jnp.float32),
            pltpu.VMEM((clusters, tokens), jnp.float32),
        ],
        compiler_params=pltpu.CompilerParams(vmem_limit_bytes=40 * 2**20),
        cost_estimate=pl.CostEstimate(
            flops=64 * ITERS * tokens * clusters * head_dim,
            bytes_accessed=tokens * head_dim * 2,
            transcendentals=ITERS * tokens * clusters,
        ),
        name="sweeps",
    )(*blocks)


def gather_rows(index, first, idx_col_ref, rows_in, out_ref):
    count, tok_dev, _ = rows_in.shape
    chunks = out_ref.shape[1] // LANES
    tokens = lax.broadcasted_iota(jnp.int32, (LANES, tok_dev), 1)

    def gather(s, carry):
        k = index ^ (s + first)
        table = pltpu.roll(idx_col_ref[...], LANES - k * chunks, 1)
        values = rows_in[s]
        for r in range(chunks):
            picks = jnp.where(tokens == table[:, r : r + 1], 1.0, 0.0).astype(jnp.bfloat16)
            out_ref[s, r * LANES : (r + 1) * LANES, :] = dot(picks, values).astype(jnp.bfloat16)
        return carry

    lax.fori_loop(0, count, gather, 0)


def position_features(index, rows_in, at):
    sources, tok_dev, _ = rows_in.shape
    shape = (tok_dev, LANES)
    token = lax.broadcasted_iota(jnp.int32, shape, 0)
    lane = lax.broadcasted_iota(jnp.int32, shape, 1)
    fine = token & (DIGIT - 1)
    for s in range(sources):
        coarse = (token + (index ^ s) * tok_dev) >> 6
        for number, columns in enumerate(
            ((1, 1, 1, coarse, fine), (coarse * DIGIT, fine, 1, -DIGIT, -1))
        ):
            feature = jnp.zeros(shape, jnp.int32)
            for place, column in enumerate(columns):
                feature = jnp.where(lane == place, column, feature)
            start = at + number * LANES
            rows_in[s, :, start : start + LANES] = feature.astype(jnp.float32).astype(jnp.bfloat16)


def gather_keys_kernel(index_ref, *refs):
    blocks, (idx_col_ref, out_ref, rows_in) = refs[:-3], refs[-3:]
    head_dim = blocks[0].shape[1]
    for s, ref in enumerate(blocks):
        rows_in[s, :, :head_dim] = ref[: rows_in.shape[1], :]
    position_features(index_ref[0], rows_in, head_dim)
    gather_rows(index_ref[0], 0, idx_col_ref, rows_in, out_ref)


def gather_near_kernel(index_ref, *refs):
    blocks, (idx_col_ref, out_ref, rows_in) = refs[:-3], refs[-3:]
    for s, ref in enumerate(blocks):
        rows_in[s] = ref[...]
    gather_rows(index_ref[0], 0, idx_col_ref, rows_in, out_ref)


def attention_kernel(segment, group, index_ref, after_ref, *refs):
    far = (len(refs) - 7) // 3
    sources = 2 * far
    blocks = refs[:far]
    near_ref, gk_ref, idx_col_ref, idx_row_ref = refs[far : far + 4]
    outs = refs[far + 4 : far + 4 + sources]
    rows_in, gathered, blended = refs[far + 4 + sources :]
    tok_dev, head_dim = rows_in.shape[1], outs[0].shape[1]
    slots = gk_ref.shape[1]
    block = sources * TILE
    scale = head_dim**-0.5 * LOG2E
    for s, ref in enumerate(blocks):
        rows_in[s] = ref[...]
    gather_rows(index_ref[0], far, idx_col_ref, rows_in, gathered)

    row_cluster = lax.broadcasted_iota(jnp.int32, (block, block), 0) % TILE // segment
    col_cluster = lax.broadcasted_iota(jnp.int32, (block, block), 1) % TILE // segment
    same = row_cluster == col_cluster
    flat = (block, head_dim)

    def attend(step, carry):
        rows = [
            pl.ds(pl.multiple_of((step * group + u) * TILE, TILE), TILE) for u in range(group)
        ]
        both = [jnp.concatenate([near_ref[:, r, :], gathered[:, r, :]], axis=0) for r in rows]
        keys = [gk_ref[:, r, :] for r in rows]

        def piece(values, number):
            at = number * head_dim
            return values[:, :, at : at + head_dim].reshape(flat)

        def against(left, right):
            return lax.dot_general(left, right, BY_ROWS, preferred_element_type=jnp.float32)

        ahead = [against(piece(k, 2), piece(k, 1)) for k in keys]
        scores = [
            jnp.where(
                same & (ahead[u] >= 1.0),
                against(piece(both[u], 0), piece(keys[u], 0)) * scale,
                -1e30,
            )
            for u in range(group)
        ]
        tops = [jnp.max(s, axis=1, keepdims=True) for s in scores]
        unnormed = [jnp.exp2(s - t) for s, t in zip(scores, tops)]
        totals = [jnp.sum(u, axis=1, keepdims=True) for u in unnormed]
        mixed = [
            dot(unnormed[u].astype(jnp.bfloat16), piece(both[u], 1))
            * (1.0 / totals[u])
            for u in range(group)
        ]
        for u in range(group):
            blended[:, rows[u], :] = (
                mixed[u].astype(jnp.bfloat16).reshape(sources, TILE, head_dim)
            )
        return carry

    lax.fori_loop(0, slots // TILE // group, attend, 0)

    tokens = lax.broadcasted_iota(jnp.int32, (tok_dev, slots), 0)
    for s in range(sources):
        wanted = idx_row_ref[pl.ds(index_ref[0] ^ s, 1), :]
        picks = jnp.where(tokens == wanted, 1.0, 0.0).astype(jnp.bfloat16)
        rows = dot(picks, blended[s]).astype(jnp.bfloat16)
        outs[s][:tok_dev, :] = rows
        wide = rows.astype(jnp.float32)
        squares = jnp.sum((wide * wide).T, axis=0, keepdims=True)
        lines = [squares[:, p : p + LANES] for p in range(0, tok_dev, LANES)]
        coarse = [line.astype(jnp.bfloat16).astype(jnp.float32) for line in lines]
        fine = [line - high for line, high in zip(lines, coarse)]
        spare = [jnp.zeros_like(lines[0])] * (TILE - 2 * len(lines))
        outs[s][tok_dev:, :] = jnp.concatenate(coarse + fine + spare, axis=0).astype(jnp.bfloat16)


def tables_kernel(tok_dev, segment, *refs):
    blocks, (idx_col_ref, idx_row_ref) = refs[:-2], refs[-2:]
    sources = len(blocks)
    width = sources * segment
    square = (LANES, LANES)
    row = lax.broadcasted_iota(jnp.int32, square, 0)
    lane = lax.broadcasted_iota(jnp.int32, square, 1)

    def ones_where(condition):
        return jnp.where(condition, 1.0, 0.0)

    spread = ones_where(row[:, :width] // segment == lane[:, :width]).astype(jnp.bfloat16)
    mine = (lane % segment == row % segment) & (lane < 2 * width)
    weight = jnp.where(row < width, float(DIGIT), 1.0) * ones_where(row < 2 * width)
    slot_of = row % width // segment
    columns = jnp.zeros(square, jnp.float32)
    by_row = (weight * ones_where(slot_of == lane))[:, :sources].T.astype(jnp.bfloat16)
    for r, block in enumerate(blocks):
        spread_digits = dot(spread, block[-width:, :])
        digits = jnp.where(mine, spread_digits, 0.0).astype(jnp.bfloat16)
        place = (lane // sources == slot_of) & (lane % sources == r)
        columns += dot(digits, (weight * ones_where(place)).astype(jnp.bfloat16))
        line = lax.dot_general(by_row, digits, BY_ROWS, preferred_element_type=jnp.float32)
        idx_row_ref[:, r * LANES : (r + 1) * LANES] = line.astype(jnp.int32) - tok_dev * row[:sources]
    idx_col_ref[...] = columns.astype(jnp.int32) - tok_dev * (lane // sources)


def run_tables(blocks, tok_dev, segment):
    sources = len(blocks)
    return pl.pallas_call(
        functools.partial(tables_kernel, tok_dev, segment),
        out_shape=(
            jax.ShapeDtypeStruct((LANES, LANES), jnp.int32),
            jax.ShapeDtypeStruct((sources, sources * LANES), jnp.int32),
        ),
        in_specs=[VMEM] * sources,
        out_specs=(VMEM, VMEM),
        compiler_params=pltpu.CompilerParams(vmem_limit_bytes=8 * 2**20),
        name="tables",
    )(*blocks)


def run_attention(index, after, key_blocks, pair_blocks, tables, tok_dev, segment, group=8):
    sources, head_dim = len(key_blocks), key_blocks[0].shape[1]
    idx_col, idx_row = tables
    slots = idx_row.shape[1]
    flops = 2 * sources * slots * tok_dev * head_dim
    gathered_keys = pl.pallas_call(
        gather_keys_kernel,
        out_shape=jax.ShapeDtypeStruct((sources, slots, 3 * head_dim), jnp.bfloat16),
        in_specs=[SMEM] + [VMEM] * (sources + 1),
        out_specs=VMEM,
        scratch_shapes=[pltpu.VMEM((sources, tok_dev, 3 * head_dim), jnp.bfloat16)],
        compiler_params=pltpu.CompilerParams(vmem_limit_bytes=24 * 2**20),
        cost_estimate=pl.CostEstimate(
            flops=4 * flops, bytes_accessed=6 * sources * tok_dev * head_dim, transcendentals=0
        ),
        name="gather_keys",
    )(index, *key_blocks, idx_col)
    near = sources // 2
    gathered_near = pl.pallas_call(
        gather_near_kernel,
        out_shape=jax.ShapeDtypeStruct((near, slots, 2 * head_dim), jnp.bfloat16),
        in_specs=[SMEM] + [VMEM] * (near + 1),
        out_specs=VMEM,
        scratch_shapes=[pltpu.VMEM((near, tok_dev, 2 * head_dim), jnp.bfloat16)],
        compiler_params=pltpu.CompilerParams(vmem_limit_bytes=24 * 2**20),
        cost_estimate=pl.CostEstimate(
            flops=4 * flops, bytes_accessed=6 * sources * tok_dev * head_dim, transcendentals=0
        ),
        name="gather_near",
    )(index, *pair_blocks[:near], idx_col)
    return pl.pallas_call(
        functools.partial(attention_kernel, segment, group),
        out_shape=[jax.ShapeDtypeStruct((tok_dev + TILE, head_dim), jnp.bfloat16)] * sources,
        in_specs=[SMEM, pl.BlockSpec(memory_space=pl.ANY)] + [VMEM] * (near + 4),
        out_specs=[VMEM] * sources,
        scratch_shapes=[
            pltpu.VMEM((near, tok_dev, 2 * head_dim), jnp.bfloat16),
            pltpu.VMEM((near, slots, 2 * head_dim), jnp.bfloat16),
            pltpu.VMEM((sources, slots, head_dim), jnp.bfloat16),
        ],
        compiler_params=pltpu.CompilerParams(vmem_limit_bytes=40 * 2**20),
        cost_estimate=pl.CostEstimate(
            flops=8 * flops,
            bytes_accessed=8 * sources * tok_dev * head_dim,
            transcendentals=slots // TILE * (sources * TILE) ** 2,
        ),
        name="attention",
    )(index, after, *pair_blocks[near:], gathered_near, gathered_keys, idx_col, idx_row)


def sum_squares_kernel(lines, *refs):
    total = sum(ref[-TILE:, :].astype(jnp.float32) for ref in refs[:-1])
    refs[-1][...] = total[:lines, :] + total[lines : 2 * lines, :]


def sum_squares(parts, tok_dev):
    lines = tok_dev // LANES
    return pl.pallas_call(
        functools.partial(sum_squares_kernel, lines),
        out_shape=jax.ShapeDtypeStruct((lines, LANES), jnp.float32),
        in_specs=[VMEM] * len(parts),
        out_specs=VMEM,
        compiler_params=pltpu.CompilerParams(vmem_limit_bytes=8 * 2**20),
        name="sum_squares",
    )(*parts)


def collect_kernel(index_ref, *refs):
    parts, (out_ref, pot_ref) = refs[:-2], refs[-2:]
    cluster_dev = out_ref.shape[1]
    for s, ref in enumerate(parts):
        head = index_ref[0] ^ s
        out_ref[head] = ref[:cluster_dev, :]
        pot_ref[pl.ds(head, 1), :] = ref[cluster_dev : cluster_dev + 1, :]


def collect(index, parts, cluster_dev):
    return pl.pallas_call(
        collect_kernel,
        out_shape=(
            jax.ShapeDtypeStruct((len(parts), cluster_dev, LANES), jnp.float32),
            jax.ShapeDtypeStruct((len(parts), LANES), jnp.float32),
        ),
        in_specs=[SMEM] + [VMEM] * len(parts),
        out_specs=(VMEM, VMEM),
        compiler_params=pltpu.CompilerParams(vmem_limit_bytes=8 * 2**20),
        name="collect",
    )(index, *parts)


def norm_kernel(width, heads, index_ref, *refs):
    parts, squares, (gain_ref, out_ref) = refs[:heads], refs[heads:-2], refs[-2:]
    head_dim = parts[0].shape[1]
    total = sum(ref[...] for ref in squares)
    inverse = lax.rsqrt(total / width + 1e-06)
    columns = [
        jnp.broadcast_to(inverse[p : p + 1, :], (LANES, LANES)).T for p in range(total.shape[0])
    ]
    for s, ref in enumerate(parts):
        head = index_ref[0] ^ s
        lanes = pl.ds(pl.multiple_of(head * head_dim, head_dim), head_dim)
        gain = gain_ref[:, lanes]
        for p, column in enumerate(columns):
            rows = slice(p * LANES, (p + 1) * LANES)
            out_ref[rows, lanes] = (ref[rows, :].astype(jnp.float32) * column * gain).astype(
                jnp.bfloat16
            )


def run_norm(index, parts, squares, gain, width, tok_dev):
    head_dim = parts[0].shape[1]
    return pl.pallas_call(
        functools.partial(norm_kernel, width, len(parts)),
        out_shape=jax.ShapeDtypeStruct((tok_dev, len(parts) * head_dim), jnp.bfloat16),
        in_specs=[SMEM] + [VMEM] * (len(parts) + len(squares) + 1),
        out_specs=VMEM,
        compiler_params=pltpu.CompilerParams(vmem_limit_bytes=24 * 2**20),
        name="norm",
    )(index, *parts, *squares, gain.reshape(1, -1))


def pack_kernel(index_ref, key_ref, centroid_ref, list_ref, count_ref, *outs):
    tok_dev = key_ref.shape[0]
    _, cluster_dev, head_dim = centroid_ref.shape
    width, sources = list_ref.shape[2], count_ref.shape[2]
    segment = width // sources
    owner = lax.broadcasted_iota(jnp.int32, (sources, width), 1) // segment
    spread = jnp.where(
        owner == lax.broadcasted_iota(jnp.int32, (sources, width), 0), 1.0, 0.0
    ).astype(jnp.bfloat16)
    slot = lax.broadcasted_iota(jnp.int32, (cluster_dev, width), 1) % segment
    at = lax.broadcasted_iota(jnp.int32, (width, head_dim), 1)
    source = lax.broadcasted_iota(jnp.int32, (width, head_dim), 0)
    first = jnp.where(at == source, 1.0, 0.0).astype(jnp.bfloat16)
    second = jnp.where(at == source + width, 1.0, 0.0).astype(jnp.bfloat16)
    for s, out in enumerate(outs):
        head = index_ref[0] ^ s
        lanes = pl.ds(pl.multiple_of(head * head_dim, head_dim), head_dim)
        out[:tok_dev, :] = key_ref[:, lanes]
        out[tok_dev : tok_dev + cluster_dev, :] = centroid_ref[head].astype(jnp.bfloat16)
        counts = dot(count_ref[head].astype(jnp.float32).astype(jnp.bfloat16), spread)
        marked = jnp.where(slot.astype(jnp.float32) < counts, list_ref[head], -TILE)
        coarse = (marked >> 6).astype(jnp.float32).astype(jnp.bfloat16)
        fine = (marked & (DIGIT - 1)).astype(jnp.float32).astype(jnp.bfloat16)
        out[tok_dev + cluster_dev :, :] = (dot(coarse, first) + dot(fine, second)).astype(
            jnp.bfloat16
        )


def pack_keys(index, key_rows, centroids, cluster_lists, live_counts):
    heads, cluster_dev, head_dim = centroids.shape
    rows = key_rows.shape[0] + 2 * cluster_dev
    return pl.pallas_call(
        pack_kernel,
        out_shape=[jax.ShapeDtypeStruct((rows, head_dim), jnp.bfloat16)] * heads,
        in_specs=[SMEM] + [VMEM] * 4,
        out_specs=[VMEM] * heads,
        compiler_params=pltpu.CompilerParams(vmem_limit_bytes=60 * 2**20),
        name="pack_keys",
    )(index, key_rows, centroids, cluster_lists, live_counts)


def shift_ring(size, step):
    return [(j, (j + step) % size) for j in range(size)]


def far_first(size):
    return list(range(size // 2, size)) + list(range(1, size // 2))


def pack_kernel(index_ref, key_ref, centroid_ref, list_ref, count_ref, *outs):
    tok_dev = key_ref.shape[0]
    _, cluster_dev, head_dim = centroid_ref.shape
    width, sources = list_ref.shape[2], count_ref.shape[2]
    segment = width // sources
    owner = lax.broadcasted_iota(jnp.int32, (sources, width), 1) // segment
    spread = jnp.where(
        owner == lax.broadcasted_iota(jnp.int32, (sources, width), 0), 1.0, 0.0
    ).astype(jnp.bfloat16)
    slot = lax.broadcasted_iota(jnp.int32, (cluster_dev, width), 1) % segment
    at = lax.broadcasted_iota(jnp.int32, (width, head_dim), 1)
    source = lax.broadcasted_iota(jnp.int32, (width, head_dim), 0)
    first = jnp.where(at == source, 1.0, 0.0).astype(jnp.bfloat16)
    second = jnp.where(at == source + width, 1.0, 0.0).astype(jnp.bfloat16)
    for s, out in enumerate(outs):
        head = index_ref[0] ^ s
        lanes = pl.ds(pl.multiple_of(head * head_dim, head_dim), head_dim)
        out[:tok_dev, :] = key_ref[:, lanes]
        out[tok_dev : tok_dev + cluster_dev, :] = centroid_ref[head].astype(jnp.bfloat16)
        counts = dot(count_ref[head].astype(jnp.float32).astype(jnp.bfloat16), spread)
        marked = jnp.where(slot.astype(jnp.float32) < counts, list_ref[head], -TILE)
        coarse = (marked >> 6).astype(jnp.float32).astype(jnp.bfloat16)
        fine = (marked & (DIGIT - 1)).astype(jnp.float32).astype(jnp.bfloat16)
        out[tok_dev + cluster_dev :, :] = (dot(coarse, first) + dot(fine, second)).astype(
            jnp.bfloat16
        )


def pack_keys(index, key_rows, centroids, cluster_lists, live_counts):
    heads, cluster_dev, head_dim = centroids.shape
    rows = key_rows.shape[0] + 2 * cluster_dev
    return pl.pallas_call(
        pack_kernel,
        out_shape=[jax.ShapeDtypeStruct((rows, head_dim), jnp.bfloat16)] * heads,
        in_specs=[SMEM] + [VMEM] * 4,
        out_specs=[VMEM] * heads,
        compiler_params=pltpu.CompilerParams(vmem_limit_bytes=60 * 2**20),
        name="pack_keys",
    )(index, key_rows, centroids, cluster_lists, live_counts)


def shift_ring(size, step):
    return [(j, (j + step) % size) for j in range(size)]


def exchange(blocks):
    size = len(blocks)
    arrived = list(blocks)
    for s in far_first(size):
        arrived[s] = lax.ppermute(blocks[s], "ctx", [(j, j ^ s) for j in range(size)])
    return arrived


def local(query_rows, key_rows, value_rows, centroids, norm_gain, cluster_lists, live_counts):
    context_length = lax.axis_size("ctx")
    head_dev = centroids.shape[0]
    if head_dev != context_length or context_length & (context_length - 1):
        return local_wide(
            query_rows, key_rows, value_rows, centroids, norm_gain, cluster_lists, live_counts
        )
    return local_heads(
        query_rows, key_rows, value_rows, centroids, norm_gain, cluster_lists, live_counts
    )


def local_heads(query_rows, key_rows, value_rows, centroids, norm_gain, cluster_lists, live_counts):
    context_length = lax.axis_size("ctx")
    head_size = lax.axis_size("head")
    tok_dev = query_rows.shape[0]
    head_dev, cluster_dev, head_dim = centroids.shape
    segment = cluster_lists.shape[2] // context_length
    index = lax.axis_index("ctx")
    place = index.astype(jnp.int32).reshape(1)

    def by_head(rows):
        return rows.reshape(tok_dev, head_dev, head_dim).transpose(1, 0, 2)

    pairs = jnp.concatenate([by_head(query_rows), by_head(value_rows)], axis=2)
    pairs = [
        lax.dynamic_index_in_dim(pairs, index ^ s, 0, keepdims=False)
        for s in range(context_length)
    ]
    key_blocks = exchange(pack_keys(place, key_rows, centroids, cluster_lists, live_counts))
    pair_blocks = exchange(pairs)
    tables = run_tables(key_blocks, tok_dev, segment)
    swept = run_sweeps(key_blocks, tok_dev, cluster_dev)
    outs = run_attention(place, swept[0], key_blocks, pair_blocks, tables, tok_dev, segment)
    parts = exchange(outs)
    swept_mine, potential_mine = collect(place, exchange(swept), cluster_dev)
    mine = sum_squares(parts, tok_dev)
    squares = [mine] + [
        lax.ppermute(mine, "head", shift_ring(head_size, step)) for step in range(1, head_size)
    ]
    features = head_dev * head_dim * head_size
    normalized = run_norm(place, parts, squares, norm_gain, features, tok_dev)
    return (normalized, swept_mine, potential_mine[:, :cluster_dev])


def solution(mesh):
    placed = (
        P("ctx", "head"),
        P("ctx", "head"),
        P("ctx", "head"),
        P("head", "ctx", None),
        P("head"),
        P("head", "ctx", None),
        P("head", "ctx", None),
    )
    return jax.shard_map(
        local,
        mesh=mesh,
        in_specs=placed,
        out_specs=(P("ctx", "head"), P("head", "ctx", None), P("head", "ctx")),
        check_vma=False,
    )
```

profile of v0, /device:TPU:0, one launch (start us, length us, event | category | flops | bytes accessed | tf_op | source)
XLA Modules:
  0.0 152.5 jit_solution(8774619693545828453)
XLA Ops:
  0.6 1.6 %copy.10.count_ref = s32[8,32,8]{2,1,0:T(8,128)} copy(s32[8,32,8]{1,2,0:T(8,128)} %param.13) | data formatting | bytes 16384 | tf_op args[6]
  2.2 2.9 %pack_keys.1 = (bf16[576,128]{1,0:T(8,128)(2,1)}, bf16[576,128]{1,0:T(8,128)(2,1)}, bf16[576,128]{1,0:T(8,128)(2,1)}, bf16[576,128]{1,0:T(8,128)(2,1)}, bf16[576...) custom-call(s32[1]{0:T(128)} %bitcast.index_ref, ...), custom_call_target="tpu_custom_call" | custom-call | tf_op jit(solution)/shard_map/pack_keys/pallas_call | solution.py:635
  5.2 3.0 %collective-permute-start = (bf16[576,128]{1,0:T(8,128)(2,1)}, bf16[576,128]{1,0:T(8,128)(2,1)S(1)}, u32[]{:S(2)}, u32[]{:S(2)}) collective-permute-start(bf16[576,128]{1,0:T(8,128)(2,1)} %get-tuple-element.32), channel_id=1, source_target_pairs={{0,4},{4,0},{8,12},{12,8},{16,20},{20,16},{24,28},{28,24},{1,5},{5... | collective-permute-start | bytes 442376 | tf_op jit(solution)/shard_map/ppermute | solution.py:653
  8.2 1.6 %collective-permute-start.1 = (bf16[576,128]{1,0:T(8,128)(2,1)}, bf16[576,128]{1,0:T(8,128)(2,1)S(1)}, u32[]{:S(2)}, u32[]{:S(2)}) collective-permute-start(bf16[576,128]{1,0:T(8,128)(2,1)} %get-tuple-element.33), channel_id=1, source_target_pairs={{0,8},{4,12},{8,0},{12,4},{16,24},{20,28},{24,16},{28,20},{1,9},{5... | collective-permute-start | bytes 442376 | tf_op jit(solution)/shard_map/ppermute | solution.py:653
  9.8 3.0 %collective-permute-start.3 = (bf16[576,128]{1,0:T(8,128)(2,1)}, bf16[576,128]{1,0:T(8,128)(2,1)S(1)}, u32[]{:S(2)}, u32[]{:S(2)}) collective-permute-start(bf16[576,128]{1,0:T(8,128)(2,1)} %get-tuple-element.35), channel_id=1, source_target_pairs={{0,16},{4,20},{8,24},{12,28},{16,0},{20,4},{24,8},{28,12},{1,17},{... | collective-permute-start | bytes 442376 | tf_op jit(solution)/shard_map/ppermute | solution.py:653
  12.7 1.3 collective-permute-start.4
  14.0 2.7 %bitcast_bitcast_fusion = (bf16[8,512,128]{2,1,0:T(8,128)(2,1)S(1)}, bf16[8,512,128]{2,1,0:T(8,128)(2,1)}) fusion(bf16[512,1024]{1,0:T(8,128)(2,1)S(1)} %copy-done, bf16[512,1024]{1,0:T(8,128)(2,1)} %param.9), kind=kLoop, calls=%fused_computation.16 | loop fusion | bytes 4194304 | tf_op jit(solution)/shard_map/transpose | solution.py:679
  16.7 1.1 fusion.8
  17.9 3.7 %collective-permute-start.5 = (bf16[576,128]{1,0:T(8,128)(2,1)S(1)}, bf16[576,128]{1,0:T(8,128)(2,1)S(1)}, u32[]{:S(2)}, u32[]{:S(2)}) collective-permute-start(bf16[576,128]{1,0:T(8,128)(2,1)S(1)} %copy-done.5), channel_id=1, source_target_pairs={{0,24},{4,28},{8,16},{12,20},{16,8},{20,12},{24,0},{28,4},{1,25},{... | collective-permute-start | bytes 442376 | tf_op jit(solution)/shard_map/ppermute | solution.py:653
  22.7 1.6 %collective-permute-start.11 = (bf16[512,256]{1,0:T(8,128)(2,1)S(1)}, bf16[512,256]{1,0:T(8,128)(2,1)S(1)}, u32[]{:S(2)}, u32[]{:S(2)}) collective-permute-start(bf16[512,256]{1,0:T(8,128)(2,1)S(1)} %get-tuple-element.66), channel_id=1, source_target_pairs={{0,4},{4,0},{8,12},{12,8},{16,20},{20,16},{24,28},{28,24},{1,5},{5... | collective-permute-start | bytes 786440 | tf_op jit(solution)/shard_map/ppermute | solution.py:653
  24.4 10.2 %collective-permute-done.4.refs_5_ = bf16[576,128]{1,0:T(8,128)(2,1)S(1)} collective-permute-done((bf16[576,128]{1,0:T(8,128)(2,1)}, bf16[576,128]{1,0:T(8,128)(2,1)S(1)}, u32[]{:S(2)}, u32[]{:S(2)}) %collective-permute-start.4) | collective-permute-done | bytes 147488 | tf_op jit(solution)/shard_map/ppermute | solution.py:653
  34.7 3.6 %collective-permute-start.10 = (bf16[512,256]{1,0:T(8,128)(2,1)S(1)}, bf16[512,256]{1,0:T(8,128)(2,1)S(1)}, u32[]{:S(2)}, u32[]{:S(2)}) collective-permute-start(bf16[512,256]{1,0:T(8,128)(2,1)S(1)} %get-tuple-element.63), channel_id=1, source_target_pairs={{0,28},{4,24},{8,20},{12,16},{16,12},{20,8},{24,4},{28,0},{1,29},{... | collective-permute-start | bytes 786440 | tf_op jit(solution)/shard_map/ppermute | solution.py:653
  38.3 16.4 %collective-permute-start.7 = (bf16[512,256]{1,0:T(8,128)(2,1)S(1)}, bf16[512,256]{1,0:T(8,128)(2,1)S(1)}, u32[]{:S(2)}, u32[]{:S(2)}) collective-permute-start(bf16[512,256]{1,0:T(8,128)(2,1)S(1)} %get-tuple-element.60), channel_id=1, source_target_pairs={{0,16},{4,20},{8,24},{12,28},{16,0},{20,4},{24,8},{28,12},{1,17},{... | collective-permute-start | bytes 786440 | tf_op jit(solution)/shard_map/ppermute | solution.py:653
  54.7 33.6 %sweeps.1 = (f32[40,128]{1,0:T(8,128)S(1)}, f32[40,128]{1,0:T(8,128)S(1)}, f32[40,128]{1,0:T(8,128)S(1)}, f32[40,128]{1,0:T(8,128)S(1)}, f32[40,128]{1,0:T(8,128...) custom-call(bf16[576,128]{1,0:T(8,128)(2,1)S(1)} %copy-done.1, ...), custom_call_target="tpu_custom_call" | custom-call | flops 42949672960 | bytes 1048576 | tf_op jit(solution)/shard_map/sweeps/pallas_call | solution.py:246
  88.3 1.1 tables.1
  89.5 8.2 %gather_keys.1.refs_5_ = bf16[8,1024,384]{2,1,0:T(8,128)(2,1)S(1)} custom-call(s32[1]{0:T(128)} %bitcast.index_ref, bf16[576,128]{1,0:T(8,128)(2,1)S(1)} %copy-done.1, bf16[576,128]{1,0:T(8,128)(2,1)S(1)} %collective-permute-done.refs_1_, bf16[576,128]{1,0:T(8,128)(2,1)S(1)} %collective-permute-done.1.refs_2_, ...), custom_call_target="tpu_custom_call" | custom-call | flops 4294967296 | bytes 3145728 | tf_op jit(solution)/shard_map/gather_keys/pallas_call | solution.py:439
  97.9 2.4 %gather_near.1.refs_4_ = bf16[4,1024,256]{2,1,0:T(8,128)(2,1)S(1)} custom-call(s32[1]{0:T(128)} %bitcast.index_ref, bf16[512,256]{1,0:T(8,128)(2,1)S(1)} %get-tuple-element.64.refs_0_, bf16[512,256]{1,0:T(8,128)(2,1)S(1)} %collective-permute-done.11.refs_1_, bf16[512,256]{1,0:T(8,128)(2,1)S(1)} %collective-permute-done.12.refs_2_, ...), custom_call_target="tpu_custom_call" | custom-call | flops 4294967296 | bytes 3145728 | tf_op jit(solution)/shard_map/gather_near/pallas_call | solution.py:452
  100.3 8.4 %collective-permute-done.8.refs_1_ = bf16[512,256]{1,0:T(8,128)(2,1)S(1)} collective-permute-done((bf16[512,256]{1,0:T(8,128)(2,1)S(1)}, bf16[512,256]{1,0:T(8,128)(2,1)S(1)}, u32[]{:S(2)}, u32[]{:S(2)}) %collective-permute-start.8) | collective-permute-done | bytes 262176 | tf_op jit(solution)/shard_map/ppermute | solution.py:653
  108.7 10.9 %attention.1 = (bf16[528,128]{1,0:T(8,128)(2,1)S(1)}, bf16[528,128]{1,0:T(8,128)(2,1)S(1)}, bf16[528,128]{1,0:T(8,128)(2,1)S(1)}, bf16[528,128]{1,0:T(8,128)(2,1...) custom-call(s32[1]{0:T(128)} %bitcast.index_ref, ...), custom_call_target="tpu_custom_call" | custom-call | flops 8589934592 | bytes 4194304 | tf_op jit(solution)/shard_map/attention/pallas_call | solution.py:464
  119.8 3.9 %collective-permute-start.15 = (bf16[528,128]{1,0:T(8,128)(2,1)S(1)}, bf16[528,128]{1,0:T(8,128)(2,1)S(1)}, u32[]{:S(2)}, u32[]{:S(2)}) collective-permute-start(bf16[528,128]{1,0:T(8,128)(2,1)S(1)} %get-tuple-element.44), channel_id=1, source_target_pairs={{0,8},{4,12},{8,0},{12,4},{16,24},{20,28},{24,16},{28,20},{1,9},{5... | collective-permute-start | bytes 405512 | tf_op jit(solution)/shard_map/ppermute | solution.py:653
  123.8 3.3 %collective-permute-start.16 = (bf16[528,128]{1,0:T(8,128)(2,1)S(1)}, bf16[528,128]{1,0:T(8,128)(2,1)S(1)}, u32[]{:S(2)}, u32[]{:S(2)}) collective-permute-start(bf16[528,128]{1,0:T(8,128)(2,1)S(1)} %get-tuple-element.45), channel_id=1, source_target_pairs={{0,12},{4,8},{8,4},{12,0},{16,28},{20,24},{24,20},{28,16},{1,13},{... | collective-permute-start | bytes 405512 | tf_op jit(solution)/shard_map/ppermute | solution.py:653
  128.6 2.4 %collective-permute-start.18 = (bf16[528,128]{1,0:T(8,128)(2,1)S(1)}, bf16[528,128]{1,0:T(8,128)(2,1)S(1)}, u32[]{:S(2)}, u32[]{:S(2)}) collective-permute-start(bf16[528,128]{1,0:T(8,128)(2,1)S(1)} %get-tuple-element.47), channel_id=1, source_target_pairs={{0,20},{4,16},{8,28},{12,24},{16,4},{20,0},{24,12},{28,8},{1,21},{... | collective-permute-start | bytes 405512 | tf_op jit(solution)/shard_map/ppermute | solution.py:653
  131.0 1.9 %collective-permute-start.19 = (bf16[528,128]{1,0:T(8,128)(2,1)S(1)}, bf16[528,128]{1,0:T(8,128)(2,1)S(1)}, u32[]{:S(2)}, u32[]{:S(2)}) collective-permute-start(bf16[528,128]{1,0:T(8,128)(2,1)S(1)} %get-tuple-element.48), channel_id=1, source_target_pairs={{0,24},{4,28},{8,16},{12,20},{16,8},{20,12},{24,0},{28,4},{1,25},{... | collective-permute-start | bytes 405512 | tf_op jit(solution)/shard_map/ppermute | solution.py:653
  133.0 2.8 %collective-permute-start.20 = (bf16[528,128]{1,0:T(8,128)(2,1)S(1)}, bf16[528,128]{1,0:T(8,128)(2,1)S(1)}, u32[]{:S(2)}, u32[]{:S(2)}) collective-permute-start(bf16[528,128]{1,0:T(8,128)(2,1)S(1)} %get-tuple-element.49), channel_id=1, source_target_pairs={{0,28},{4,24},{8,20},{12,16},{16,12},{20,8},{24,4},{28,0},{1,29},{... | collective-permute-start | bytes 405512 | tf_op jit(solution)/shard_map/ppermute | solution.py:653
  135.8 2.6 %collective-permute-done.17.refs_4_ = bf16[528,128]{1,0:T(8,128)(2,1)S(1)} collective-permute-done((bf16[528,128]{1,0:T(8,128)(2,1)S(1)}, bf16[528,128]{1,0:T(8,128)(2,1)S(1)}, u32[]{:S(2)}, u32[]{:S(2)}) %collective-permute-start.17) | collective-permute-done | bytes 135200 | tf_op jit(solution)/shard_map/ppermute | solution.py:653
  138.4 3.5 %collective-permute-done.18.refs_5_ = bf16[528,128]{1,0:T(8,128)(2,1)S(1)} collective-permute-done((bf16[528,128]{1,0:T(8,128)(2,1)S(1)}, bf16[528,128]{1,0:T(8,128)(2,1)S(1)}, u32[]{:S(2)}, u32[]{:S(2)}) %collective-permute-start.18) | collective-permute-done | bytes 135200 | tf_op jit(solution)/shard_map/ppermute | solution.py:653
  141.9 1.9 %collective-permute-start.29 = (f32[40,128]{1,0:T(8,128)S(1)}, f32[40,128]{1,0:T(8,128)S(1)}, u32[]{:S(2)}, u32[]{:S(2)}) collective-permute-start(f32[40,128]{1,0:T(8,128)S(1)} %get-tuple-element.55), channel_id=1, source_target_pairs={{0,24},{4,28},{8,16},{12,20},{16,8},{20,12},{24,0},{28,4},{1,25},{... | collective-permute-start | bytes 61448 | tf_op jit(solution)/shard_map/ppermute | solution.py:653
  143.8 2.3 %collective-permute-start.30 = (f32[40,128]{1,0:T(8,128)S(1)}, f32[40,128]{1,0:T(8,128)S(1)}, u32[]{:S(2)}, u32[]{:S(2)}) collective-permute-start(f32[40,128]{1,0:T(8,128)S(1)} %get-tuple-element.56), channel_id=1, source_target_pairs={{0,28},{4,24},{8,20},{12,16},{16,12},{20,8},{24,4},{28,0},{1,29},{... | collective-permute-start | bytes 61448 | tf_op jit(solution)/shard_map/ppermute | solution.py:653
  146.2 1.6 %collective-permute-start.22 = (f32[4,128]{1,0:T(4,128)S(1)}, f32[4,128]{1,0:T(4,128)S(1)}, u32[]{:S(2)}, u32[]{:S(2)}) collective-permute-start(f32[4,128]{1,0:T(4,128)S(1)} %sum_squares.1.refs_8_), channel_id=1, source_target_pairs={{0,2},{1,3},{2,0},{3,1},{4,6},{5,7},{6,4},{7,5},{8,10},{9,11},{10,... | collective-permute-start | bytes 6152 | tf_op jit(solution)/shard_map/ppermute | solution.py:695
  147.8 1.4 collective-permute-start.23
  149.2 1.2 collective-permute-done.30.refs_7_
  151.0 1.5 norm.1
  (55 shorter events, 3.9 us)
Async XLA Ops:
  5.2 12.7 %collective-permute-start = (bf16[576,128]{1,0:T(8,128)(2,1)}, bf16[576,128]{1,0:T(8,128)(2,1)S(1)}, u32[]{:S(2)}, u32[]{:S(2)}) collective-permute-start(bf16[576,128]{1,0:T(8,128)(2,1)} %get-tuple-element.32), channel_id=1, source_target_pairs={{0,4},{4,0},{8,12},{12,8},{16,20},{20,16},{24,28},{28,24},{1,5},{5... | collective-permute-start | bytes 442376 | tf_op jit(solution)/shard_map/ppermute | solution.py:653
  8.2 13.4 %collective-permute-start.1 = (bf16[576,128]{1,0:T(8,128)(2,1)}, bf16[576,128]{1,0:T(8,128)(2,1)S(1)}, u32[]{:S(2)}, u32[]{:S(2)}) collective-permute-start(bf16[576,128]{1,0:T(8,128)(2,1)} %get-tuple-element.33), channel_id=1, source_target_pairs={{0,8},{4,12},{8,0},{12,4},{16,24},{20,28},{24,16},{28,20},{1,9},{5... | collective-permute-start | bytes 442376 | tf_op jit(solution)/shard_map/ppermute | solution.py:653
  9.8 12.1 %collective-permute-start.2 = (bf16[576,128]{1,0:T(8,128)(2,1)}, bf16[576,128]{1,0:T(8,128)(2,1)S(1)}, u32[]{:S(2)}, u32[]{:S(2)}) collective-permute-start(bf16[576,128]{1,0:T(8,128)(2,1)} %get-tuple-element.34), channel_id=1, source_target_pairs={{0,12},{4,8},{8,4},{12,0},{16,28},{20,24},{24,20},{28,16},{1,13},{... | collective-permute-start | bytes 442376 | tf_op jit(solution)/shard_map/ppermute | solution.py:653
  9.8 13.0 %collective-permute-start.3 = (bf16[576,128]{1,0:T(8,128)(2,1)}, bf16[576,128]{1,0:T(8,128)(2,1)S(1)}, u32[]{:S(2)}, u32[]{:S(2)}) collective-permute-start(bf16[576,128]{1,0:T(8,128)(2,1)} %get-tuple-element.35), channel_id=1, source_target_pairs={{0,16},{4,20},{8,24},{12,28},{16,0},{20,4},{24,8},{28,12},{1,17},{... | collective-permute-start | bytes 442376 | tf_op jit(solution)/shard_map/ppermute | solution.py:653
  12.7 21.9 %collective-permute-start.4 = (bf16[576,128]{1,0:T(8,128)(2,1)}, bf16[576,128]{1,0:T(8,128)(2,1)S(1)}, u32[]{:S(2)}, u32[]{:S(2)}) collective-permute-start(bf16[576,128]{1,0:T(8,128)(2,1)} %get-tuple-element.36), channel_id=1, source_target_pairs={{0,20},{4,16},{8,28},{12,24},{16,4},{20,0},{24,12},{28,8},{1,21},{... | collective-permute-start | bytes 442376 | tf_op jit(solution)/shard_map/ppermute | solution.py:653
  17.9 16.8 %collective-permute-start.5 = (bf16[576,128]{1,0:T(8,128)(2,1)S(1)}, bf16[576,128]{1,0:T(8,128)(2,1)S(1)}, u32[]{:S(2)}, u32[]{:S(2)}) collective-permute-start(bf16[576,128]{1,0:T(8,128)(2,1)S(1)} %copy-done.5), channel_id=1, source_target_pairs={{0,24},{4,28},{8,16},{12,20},{16,8},{20,12},{24,0},{28,4},{1,25},{... | collective-permute-start | bytes 442376 | tf_op jit(solution)/shard_map/ppermute | solution.py:653
  21.6 16.7 %collective-permute-start.6 = (bf16[576,128]{1,0:T(8,128)(2,1)S(1)}, bf16[576,128]{1,0:T(8,128)(2,1)S(1)}, u32[]{:S(2)}, u32[]{:S(2)}) collective-permute-start(bf16[576,128]{1,0:T(8,128)(2,1)S(1)} %copy-done.4), channel_id=1, source_target_pairs={{0,28},{4,24},{8,20},{12,16},{16,12},{20,8},{24,4},{28,0},{1,29},{... | collective-permute-start | bytes 442376 | tf_op jit(solution)/shard_map/ppermute | solution.py:653
  21.8 75.9 %collective-permute-start.13 = (bf16[512,256]{1,0:T(8,128)(2,1)S(1)}, bf16[512,256]{1,0:T(8,128)(2,1)S(1)}, u32[]{:S(2)}, u32[]{:S(2)}) collective-permute-start(bf16[512,256]{1,0:T(8,128)(2,1)S(1)} %get-tuple-element.59), channel_id=1, source_target_pairs={{0,12},{4,8},{8,4},{12,0},{16,28},{20,24},{24,20},{28,16},{1,13},{... | collective-permute-start | bytes 786440 | tf_op jit(solution)/shard_map/ppermute | solution.py:653
  22.7 75.0 %collective-permute-start.11 = (bf16[512,256]{1,0:T(8,128)(2,1)S(1)}, bf16[512,256]{1,0:T(8,128)(2,1)S(1)}, u32[]{:S(2)}, u32[]{:S(2)}) collective-permute-start(bf16[512,256]{1,0:T(8,128)(2,1)S(1)} %get-tuple-element.66), channel_id=1, source_target_pairs={{0,4},{4,0},{8,12},{12,8},{16,20},{20,16},{24,28},{28,24},{1,5},{5... | collective-permute-start | bytes 786440 | tf_op jit(solution)/shard_map/ppermute | solution.py:653
  34.6 63.3 %collective-permute-start.12 = (bf16[512,256]{1,0:T(8,128)(2,1)S(1)}, bf16[512,256]{1,0:T(8,128)(2,1)S(1)}, u32[]{:S(2)}, u32[]{:S(2)}) collective-permute-start(bf16[512,256]{1,0:T(8,128)(2,1)S(1)} %get-tuple-element.65), channel_id=1, source_target_pairs={{0,8},{4,12},{8,0},{12,4},{16,24},{20,28},{24,16},{28,20},{1,9},{5... | collective-permute-start | bytes 786440 | tf_op jit(solution)/shard_map/ppermute | solution.py:653
  34.7 65.6 %collective-permute-start.10 = (bf16[512,256]{1,0:T(8,128)(2,1)S(1)}, bf16[512,256]{1,0:T(8,128)(2,1)S(1)}, u32[]{:S(2)}, u32[]{:S(2)}) collective-permute-start(bf16[512,256]{1,0:T(8,128)(2,1)S(1)} %get-tuple-element.63), channel_id=1, source_target_pairs={{0,28},{4,24},{8,20},{12,16},{16,12},{20,8},{24,4},{28,0},{1,29},{... | collective-permute-start | bytes 786440 | tf_op jit(solution)/shard_map/ppermute | solution.py:653
  38.3 62.0 %collective-permute-start.7 = (bf16[512,256]{1,0:T(8,128)(2,1)S(1)}, bf16[512,256]{1,0:T(8,128)(2,1)S(1)}, u32[]{:S(2)}, u32[]{:S(2)}) collective-permute-start(bf16[512,256]{1,0:T(8,128)(2,1)S(1)} %get-tuple-element.60), channel_id=1, source_target_pairs={{0,16},{4,20},{8,24},{12,28},{16,0},{20,4},{24,8},{28,12},{1,17},{... | collective-permute-start | bytes 786440 | tf_op jit(solution)/shard_map/ppermute | solution.py:653
  97.7 11.0 %collective-permute-start.8 = (bf16[512,256]{1,0:T(8,128)(2,1)S(1)}, bf16[512,256]{1,0:T(8,128)(2,1)S(1)}, u32[]{:S(2)}, u32[]{:S(2)}) collective-permute-start(bf16[512,256]{1,0:T(8,128)(2,1)S(1)} %get-tuple-element.61), channel_id=1, source_target_pairs={{0,20},{4,16},{8,28},{12,24},{16,4},{20,0},{24,12},{28,8},{1,21},{... | collective-permute-start | bytes 786440 | tf_op jit(solution)/shard_map/ppermute | solution.py:653
  97.8 11.0 %collective-permute-start.9 = (bf16[512,256]{1,0:T(8,128)(2,1)S(1)}, bf16[512,256]{1,0:T(8,128)(2,1)S(1)}, u32[]{:S(2)}, u32[]{:S(2)}) collective-permute-start(bf16[512,256]{1,0:T(8,128)(2,1)S(1)} %get-tuple-element.62), channel_id=1, source_target_pairs={{0,24},{4,28},{8,16},{12,20},{16,8},{20,12},{24,0},{28,4},{1,25},{... | collective-permute-start | bytes 786440 | tf_op jit(solution)/shard_map/ppermute | solution.py:653
  108.7 42.2 %copy-start.2 = (f32[1024]{0:T(1024)S(1)}, f32[1024]{0:T(1024)}, u32[]{:S(2)}) copy-start(f32[1024]{0:T(1024)} %param.11) | copy-start | bytes 12292
  119.7 11.3 %collective-permute-start.14 = (bf16[528,128]{1,0:T(8,128)(2,1)S(1)}, bf16[528,128]{1,0:T(8,128)(2,1)S(1)}, u32[]{:S(2)}, u32[]{:S(2)}) collective-permute-start(bf16[528,128]{1,0:T(8,128)(2,1)S(1)} %get-tuple-element.43), channel_id=1, source_target_pairs={{0,4},{4,0},{8,12},{12,8},{16,20},{20,16},{24,28},{28,24},{1,5},{5... | collective-permute-start | bytes 405512 | tf_op jit(solution)/shard_map/ppermute | solution.py:653
  119.8 13.2 %collective-permute-start.15 = (bf16[528,128]{1,0:T(8,128)(2,1)S(1)}, bf16[528,128]{1,0:T(8,128)(2,1)S(1)}, u32[]{:S(2)}, u32[]{:S(2)}) collective-permute-start(bf16[528,128]{1,0:T(8,128)(2,1)S(1)} %get-tuple-element.44), channel_id=1, source_target_pairs={{0,8},{4,12},{8,0},{12,4},{16,24},{20,28},{24,16},{28,20},{1,9},{5... | collective-permute-start | bytes 405512 | tf_op jit(solution)/shard_map/ppermute | solution.py:653
  123.7 4.4 %collective-permute-start.24 = (f32[40,128]{1,0:T(8,128)S(1)}, f32[40,128]{1,0:T(8,128)S(1)}, u32[]{:S(2)}, u32[]{:S(2)}) collective-permute-start(f32[40,128]{1,0:T(8,128)S(1)} %get-tuple-element.50), channel_id=1, source_target_pairs={{0,4},{4,0},{8,12},{12,8},{16,20},{20,16},{24,28},{28,24},{1,5},{5... | collective-permute-start | bytes 61448 | tf_op jit(solution)/shard_map/ppermute | solution.py:653
  123.8 4.9 %collective-permute-start.25 = (f32[40,128]{1,0:T(8,128)S(1)}, f32[40,128]{1,0:T(8,128)S(1)}, u32[]{:S(2)}, u32[]{:S(2)}) collective-permute-start(f32[40,128]{1,0:T(8,128)S(1)} %get-tuple-element.51), channel_id=1, source_target_pairs={{0,8},{4,12},{8,0},{12,4},{16,24},{20,28},{24,16},{28,20},{1,9},{5... | collective-permute-start | bytes 61448 | tf_op jit(solution)/shard_map/ppermute | solution.py:653
  123.8 11.9 %collective-permute-start.16 = (bf16[528,128]{1,0:T(8,128)(2,1)S(1)}, bf16[528,128]{1,0:T(8,128)(2,1)S(1)}, u32[]{:S(2)}, u32[]{:S(2)}) collective-permute-start(bf16[528,128]{1,0:T(8,128)(2,1)S(1)} %get-tuple-element.45), channel_id=1, source_target_pairs={{0,12},{4,8},{8,4},{12,0},{16,28},{20,24},{24,20},{28,16},{1,13},{... | collective-permute-start | bytes 405512 | tf_op jit(solution)/shard_map/ppermute | solution.py:653
  128.1 10.3 %collective-permute-start.17 = (bf16[528,128]{1,0:T(8,128)(2,1)S(1)}, bf16[528,128]{1,0:T(8,128)(2,1)S(1)}, u32[]{:S(2)}, u32[]{:S(2)}) collective-permute-start(bf16[528,128]{1,0:T(8,128)(2,1)S(1)} %get-tuple-element.46), channel_id=1, source_target_pairs={{0,16},{4,20},{8,24},{12,28},{16,0},{20,4},{24,8},{28,12},{1,17},{... | collective-permute-start | bytes 405512 | tf_op jit(solution)/shard_map/ppermute | solution.py:653
  128.6 13.3 %collective-permute-start.18 = (bf16[528,128]{1,0:T(8,128)(2,1)S(1)}, bf16[528,128]{1,0:T(8,128)(2,1)S(1)}, u32[]{:S(2)}, u32[]{:S(2)}) collective-permute-start(bf16[528,128]{1,0:T(8,128)(2,1)S(1)} %get-tuple-element.47), channel_id=1, source_target_pairs={{0,20},{4,16},{8,28},{12,24},{16,4},{20,0},{24,12},{28,8},{1,21},{... | collective-permute-start | bytes 405512 | tf_op jit(solution)/shard_map/ppermute | solution.py:653
  131.0 10.9 %collective-permute-start.19 = (bf16[528,128]{1,0:T(8,128)(2,1)S(1)}, bf16[528,128]{1,0:T(8,128)(2,1)S(1)}, u32[]{:S(2)}, u32[]{:S(2)}) collective-permute-start(bf16[528,128]{1,0:T(8,128)(2,1)S(1)} %get-tuple-element.48), channel_id=1, source_target_pairs={{0,24},{4,28},{8,16},{12,20},{16,8},{20,12},{24,0},{28,4},{1,25},{... | collective-permute-start | bytes 405512 | tf_op jit(solution)/shard_map/ppermute | solution.py:653
  133.0 10.9 %collective-permute-start.20 = (bf16[528,128]{1,0:T(8,128)(2,1)S(1)}, bf16[528,128]{1,0:T(8,128)(2,1)S(1)}, u32[]{:S(2)}, u32[]{:S(2)}) collective-permute-start(bf16[528,128]{1,0:T(8,128)(2,1)S(1)} %get-tuple-element.49), channel_id=1, source_target_pairs={{0,28},{4,24},{8,20},{12,16},{16,12},{20,8},{24,4},{28,0},{1,29},{... | collective-permute-start | bytes 405512 | tf_op jit(solution)/shard_map/ppermute | solution.py:653
  135.8 10.4 %collective-permute-start.26 = (f32[40,128]{1,0:T(8,128)S(1)}, f32[40,128]{1,0:T(8,128)S(1)}, u32[]{:S(2)}, u32[]{:S(2)}) collective-permute-start(f32[40,128]{1,0:T(8,128)S(1)} %get-tuple-element.52), channel_id=1, source_target_pairs={{0,12},{4,8},{8,4},{12,0},{16,28},{20,24},{24,20},{28,16},{1,13},{... | collective-permute-start | bytes 61448 | tf_op jit(solution)/shard_map/ppermute | solution.py:653
  138.4 7.8 %collective-permute-start.27 = (f32[40,128]{1,0:T(8,128)S(1)}, f32[40,128]{1,0:T(8,128)S(1)}, u32[]{:S(2)}, u32[]{:S(2)}) collective-permute-start(f32[40,128]{1,0:T(8,128)S(1)} %get-tuple-element.53), channel_id=1, source_target_pairs={{0,16},{4,20},{8,24},{12,28},{16,0},{20,4},{24,8},{28,12},{1,17},{... | collective-permute-start | bytes 61448 | tf_op jit(solution)/shard_map/ppermute | solution.py:653
  141.9 5.9 %collective-permute-start.28 = (f32[40,128]{1,0:T(8,128)S(1)}, f32[40,128]{1,0:T(8,128)S(1)}, u32[]{:S(2)}, u32[]{:S(2)}) collective-permute-start(f32[40,128]{1,0:T(8,128)S(1)} %get-tuple-element.54), channel_id=1, source_target_pairs={{0,20},{4,16},{8,28},{12,24},{16,4},{20,0},{24,12},{28,8},{1,21},{... | collective-permute-start | bytes 61448 | tf_op jit(solution)/shard_map/ppermute | solution.py:653
  141.9 7.2 %collective-permute-start.29 = (f32[40,128]{1,0:T(8,128)S(1)}, f32[40,128]{1,0:T(8,128)S(1)}, u32[]{:S(2)}, u32[]{:S(2)}) collective-permute-start(f32[40,128]{1,0:T(8,128)S(1)} %get-tuple-element.55), channel_id=1, source_target_pairs={{0,24},{4,28},{8,16},{12,20},{16,8},{20,12},{24,0},{28,4},{1,25},{... | collective-permute-start | bytes 61448 | tf_op jit(solution)/shard_map/ppermute | solution.py:653
  143.8 6.5 %collective-permute-start.30 = (f32[40,128]{1,0:T(8,128)S(1)}, f32[40,128]{1,0:T(8,128)S(1)}, u32[]{:S(2)}, u32[]{:S(2)}) collective-permute-start(f32[40,128]{1,0:T(8,128)S(1)} %get-tuple-element.56), channel_id=1, source_target_pairs={{0,28},{4,24},{8,20},{12,16},{16,12},{20,8},{24,4},{28,0},{1,29},{... | collective-permute-start | bytes 61448 | tf_op jit(solution)/shard_map/ppermute | solution.py:653
  146.1 4.8 %collective-permute-start.21 = (f32[4,128]{1,0:T(4,128)S(1)}, f32[4,128]{1,0:T(4,128)S(1)}, u32[]{:S(2)}, u32[]{:S(2)}) collective-permute-start(f32[4,128]{1,0:T(4,128)S(1)} %sum_squares.1.refs_8_), channel_id=1, source_target_pairs={{0,1},{1,2},{2,3},{3,0},{4,5},{5,6},{6,7},{7,4},{8,9},{9,10},{10,1... | collective-permute-start | bytes 6152 | tf_op jit(solution)/shard_map/ppermute | solution.py:695
  146.2 4.8 %collective-permute-start.22 = (f32[4,128]{1,0:T(4,128)S(1)}, f32[4,128]{1,0:T(4,128)S(1)}, u32[]{:S(2)}, u32[]{:S(2)}) collective-permute-start(f32[4,128]{1,0:T(4,128)S(1)} %sum_squares.1.refs_8_), channel_id=1, source_target_pairs={{0,2},{1,3},{2,0},{3,1},{4,6},{5,7},{6,4},{7,5},{8,10},{9,11},{10,... | collective-permute-start | bytes 6152 | tf_op jit(solution)/shard_map/ppermute | solution.py:695
  147.8 3.2 %collective-permute-start.23 = (f32[4,128]{1,0:T(4,128)S(1)}, f32[4,128]{1,0:T(4,128)S(1)}, u32[]{:S(2)}, u32[]{:S(2)}) collective-permute-start(f32[4,128]{1,0:T(4,128)S(1)} %sum_squares.1.refs_8_), channel_id=1, source_target_pairs={{0,3},{1,0},{2,1},{3,2},{4,7},{5,4},{6,5},{7,6},{8,11},{9,8},{10,9... | collective-permute-start | bytes 6152 | tf_op jit(solution)/shard_map/ppermute | solution.py:695
  (5 other events, 61.1 us)
where the time goes:
time: 153 us
  Pallas kernels  61.4 us (40%)
  starting transfers between devices  57.2 us (37%)
  waiting for transfers between devices  27.5 us (18%)
  local copies, waits for them, and re-layouts  4.34 us (3%)
    ppermute x28, starting transfers between devices, exchange(): lax.ppermute(blocks[s], 'ctx', [(j, j ^ s) for j in range(size)])  54.2 us
    pallas_call x1, Pallas kernels, run_sweeps(): pl.pallas_call(functools.partial(sweeps_kernel, tok_dev, cluster_dev), ou...  33.6 us
    ppermute x28, waiting for transfers between devices, exchange(): lax.ppermute(blocks[s], 'ctx', [(j, j ^ s) for j in range(size)])  27.5 us
    pallas_call x1, Pallas kernels, run_attention(): pl.pallas_call(functools.partial(attention_kernel, segment, group), out_s...  10.9 us
    pallas_call x1, Pallas kernels, run_attention(): pl.pallas_call(gather_keys_kernel, out_shape=jax.ShapeDtypeStruct((source...  8.23 us
  transfers between devices with their start and end apart: 31, of which 7 were waited for; matrix products, arithmetic and copies ran while one was open for 3% of the time, Pallas kernels for 30%

commit v1 on v0

--- a/solution.py
+++ b/solution.py
@@ -555,7 +555,7 @@
 def pack_kernel(index_ref, key_ref, centroid_ref, list_ref, count_ref, *outs):
     tok_dev = key_ref.shape[0]
     _, cluster_dev, head_dim = centroid_ref.shape
-    width, sources = list_ref.shape[2], count_ref.shape[2]
+    width, sources = list_ref.shape[2], count_ref.shape[1]
     segment = width // sources
     owner = lax.broadcasted_iota(jnp.int32, (sources, width), 1) // segment
     spread = jnp.where(
@@ -571,7 +571,10 @@
         lanes = pl.ds(pl.multiple_of(head * head_dim, head_dim), head_dim)
         out[:tok_dev, :] = key_ref[:, lanes]
         out[tok_dev : tok_dev + cluster_dev, :] = centroid_ref[head].astype(jnp.bfloat16)
-        counts = dot(count_ref[head].astype(jnp.float32).astype(jnp.bfloat16), spread)
+        counts = lax.dot_general(
+            count_ref[head].astype(jnp.float32).astype(jnp.bfloat16), spread,
+            (((0,), (0,)), ((), ())), preferred_element_type=jnp.float32,
+        )
         marked = jnp.where(slot.astype(jnp.float32) < counts, list_ref[head], -TILE)
         coarse = (marked >> 6).astype(jnp.float32).astype(jnp.bfloat16)
         fine = (marked & (DIGIT - 1)).astype(jnp.float32).astype(jnp.bfloat16)
@@ -590,7 +593,7 @@
         out_specs=[VMEM] * heads,
         compiler_params=pltpu.CompilerParams(vmem_limit_bytes=60 * 2**20),
         name="pack_keys",
-    )(index, key_rows, centroids, cluster_lists, live_counts)
+    )(index, key_rows, centroids, cluster_lists, live_counts.transpose(0, 2, 1))
 
 
 def shift_ring(size, step):
@@ -604,7 +607,7 @@
 def pack_kernel(index_ref, key_ref, centroid_ref, list_ref, count_ref, *outs):
     tok_dev = key_ref.shape[0]
     _, cluster_dev, head_dim = centroid_ref.shape
-    width, sources = list_ref.shape[2], count_ref.shape[2]
+    width, sources = list_ref.shape[2], count_ref.shape[1]
     segment = width // sources
     owner = lax.broadcasted_iota(jnp.int32, (sources, width), 1) // segment
     spread = jnp.where(
@@ -620,7 +623,10 @@
         lanes = pl.ds(pl.multiple_of(head * head_dim, head_dim), head_dim)
         out[:tok_dev, :] = key_ref[:, lanes]
         out[tok_dev : tok_dev + cluster_dev, :] = centroid_ref[head].astype(jnp.bfloat16)
-        counts = dot(count_ref[head].astype(jnp.float32).astype(jnp.bfloat16), spread)
+        counts = lax.dot_general(
+            count_ref[head].astype(jnp.float32).astype(jnp.bfloat16), spread,
+            (((0,), (0,)), ((), ())), preferred_element_type=jnp.float32,
+        )
         marked = jnp.where(slot.astype(jnp.float32) < counts, list_ref[head], -TILE)
         coarse = (marked >> 6).astype(jnp.float32).astype(jnp.bfloat16)
         fine = (marked & (DIGIT - 1)).astype(jnp.float32).astype(jnp.bfloat16)
@@ -639,7 +645,7 @@
         out_specs=[VMEM] * heads,
         compiler_params=pltpu.CompilerParams(vmem_limit_bytes=60 * 2**20),
         name="pack_keys",
-    )(index, key_rows, centroids, cluster_lists, live_counts)
+    )(index, key_rows, centroids, cluster_lists, live_counts.transpose(0, 2, 1))
 
 
 def shift_ring(size, step):

time: 153 us -> 155 us (1.013)
  waiting for transfers between devices: 27.5 us -> 29.7 us
  local copies, waits for them, and re-layouts: 4.34 us -> 2.74 us
    ppermute x28, starting transfers between devices: 54.2 us -> 56.3 us  [exchange(): lax.ppermute(blocks[s], 'ctx', [(j, j ^ s) for j in range(size)])]
    ppermute x28, waiting for transfers between devices: 27.5 us -> 29.4 us  [exchange(): lax.ppermute(blocks[s], 'ctx', [(j, j ^ s) for j in range(size)])]
    unnamed x13 -> x12, local copies, waits for them, and re-layouts: 1.63 us -> 0.03 us
where the time goes in v1:
time: 155 us; the launch traced here: 154 us
  Pallas kernels  61.6 us (40%)
  starting transfers between devices  58.2 us (38%)
  waiting for transfers between devices  29.7 us (19%)
  local copies, waits for them, and re-layouts  2.74 us (2%)
    ppermute x28, starting transfers between devices, exchange(): lax.ppermute(blocks[s], 'ctx', [(j, j ^ s) for j in range(size)])  56.3 us
    pallas_call x1, Pallas kernels, run_sweeps(): pl.pallas_call(functools.partial(sweeps_kernel, tok_dev, cluster_dev), ou...  33.8 us
    ppermute x28, waiting for transfers between devices, exchange(): lax.ppermute(blocks[s], 'ctx', [(j, j ^ s) for j in range(size)])  29.4 us
    pallas_call x1, Pallas kernels, run_attention(): pl.pallas_call(functools.partial(attention_kernel, segment, group), out_s...  10.9 us
    pallas_call x1, Pallas kernels, run_attention(): pl.pallas_call(gather_keys_kernel, out_shape=jax.ShapeDtypeStruct((source...  8.23 us
  transfers between devices with their start and end apart: 31, of which 7 were waited for; matrix products, arithmetic and copies ran while one was open for 3% of the time, Pallas kernels for 30%

profile of v1, /device:TPU:0, one launch (start us, length us, event | category | flops | bytes accessed | tf_op | source)
XLA Modules:
  0.0 154.4 jit_solution(14375041824743294628)
XLA Ops:
  0.7 3.0 %pack_keys.1 = (bf16[576,128]{1,0:T(8,128)(2,1)}, bf16[576,128]{1,0:T(8,128)(2,1)}, bf16[576,128]{1,0:T(8,128)(2,1)}, bf16[576,128]{1,0:T(8,128)(2,1)}, bf16[576...) custom-call(s32[1]{0:T(128)} %bitcast.index_ref, ...), custom_call_target="tpu_custom_call" | custom-call | tf_op jit(solution)/shard_map/pack_keys/pallas_call | solution.py:641
  3.7 3.0 %collective-permute-start = (bf16[576,128]{1,0:T(8,128)(2,1)}, bf16[576,128]{1,0:T(8,128)(2,1)S(1)}, u32[]{:S(2)}, u32[]{:S(2)}) collective-permute-start(bf16[576,128]{1,0:T(8,128)(2,1)} %get-tuple-element.32), channel_id=1, source_target_pairs={{0,4},{4,0},{8,12},{12,8},{16,20},{20,16},{24,28},{28,24},{1,5},{5... | collective-permute-start | bytes 442376 | tf_op jit(solution)/shard_map/ppermute | solution.py:659
  6.7 1.6 %collective-permute-start.1 = (bf16[576,128]{1,0:T(8,128)(2,1)}, bf16[576,128]{1,0:T(8,128)(2,1)S(1)}, u32[]{:S(2)}, u32[]{:S(2)}) collective-permute-start(bf16[576,128]{1,0:T(8,128)(2,1)} %get-tuple-element.33), channel_id=1, source_target_pairs={{0,8},{4,12},{8,0},{12,4},{16,24},{20,28},{24,16},{28,20},{1,9},{5... | collective-permute-start | bytes 442376 | tf_op jit(solution)/shard_map/ppermute | solution.py:659
  8.2 3.0 %collective-permute-start.3 = (bf16[576,128]{1,0:T(8,128)(2,1)}, bf16[576,128]{1,0:T(8,128)(2,1)S(1)}, u32[]{:S(2)}, u32[]{:S(2)}) collective-permute-start(bf16[576,128]{1,0:T(8,128)(2,1)} %get-tuple-element.35), channel_id=1, source_target_pairs={{0,16},{4,20},{8,24},{12,28},{16,0},{20,4},{24,8},{28,12},{1,17},{... | collective-permute-start | bytes 442376 | tf_op jit(solution)/shard_map/ppermute | solution.py:659
  11.2 1.3 collective-permute-start.4
  12.5 2.7 %bitcast_bitcast_fusion = (bf16[8,512,128]{2,1,0:T(8,128)(2,1)S(1)}, bf16[8,512,128]{2,1,0:T(8,128)(2,1)}) fusion(bf16[512,1024]{1,0:T(8,128)(2,1)S(1)} %copy-done, bf16[512,1024]{1,0:T(8,128)(2,1)} %param.9), kind=kLoop, calls=%fused_computation.16 | loop fusion | bytes 4194304 | tf_op jit(solution)/shard_map/transpose | solution.py:685
  15.2 1.1 fusion.8
  16.4 3.7 %collective-permute-start.5 = (bf16[576,128]{1,0:T(8,128)(2,1)S(1)}, bf16[576,128]{1,0:T(8,128)(2,1)S(1)}, u32[]{:S(2)}, u32[]{:S(2)}) collective-permute-start(bf16[576,128]{1,0:T(8,128)(2,1)S(1)} %copy-done.5), channel_id=1, source_target_pairs={{0,24},{4,28},{8,16},{12,20},{16,8},{20,12},{24,0},{28,4},{1,25},{... | collective-permute-start | bytes 442376 | tf_op jit(solution)/shard_map/ppermute | solution.py:659
  20.7 2.2 %collective-permute-start.11 = (bf16[512,256]{1,0:T(8,128)(2,1)S(1)}, bf16[512,256]{1,0:T(8,128)(2,1)S(1)}, u32[]{:S(2)}, u32[]{:S(2)}) collective-permute-start(bf16[512,256]{1,0:T(8,128)(2,1)S(1)} %get-tuple-element.66), channel_id=1, source_target_pairs={{0,4},{4,0},{8,12},{12,8},{16,20},{20,16},{24,28},{28,24},{1,5},{5... | collective-permute-start | bytes 786440 | tf_op jit(solution)/shard_map/ppermute | solution.py:659
  22.9 10.2 %collective-permute-done.4.refs_5_ = bf16[576,128]{1,0:T(8,128)(2,1)S(1)} collective-permute-done((bf16[576,128]{1,0:T(8,128)(2,1)}, bf16[576,128]{1,0:T(8,128)(2,1)S(1)}, u32[]{:S(2)}, u32[]{:S(2)}) %collective-permute-start.4) | collective-permute-done | bytes 147488 | tf_op jit(solution)/shard_map/ppermute | solution.py:659
  33.9 4.3 %collective-permute-start.7 = (bf16[512,256]{1,0:T(8,128)(2,1)S(1)}, bf16[512,256]{1,0:T(8,128)(2,1)S(1)}, u32[]{:S(2)}, u32[]{:S(2)}) collective-permute-start(bf16[512,256]{1,0:T(8,128)(2,1)S(1)} %get-tuple-element.60), channel_id=1, source_target_pairs={{0,16},{4,20},{8,24},{12,28},{16,0},{20,4},{24,8},{28,12},{1,17},{... | collective-permute-start | bytes 786440 | tf_op jit(solution)/shard_map/ppermute | solution.py:659
  38.2 4.7 %collective-permute-start.8 = (bf16[512,256]{1,0:T(8,128)(2,1)S(1)}, bf16[512,256]{1,0:T(8,128)(2,1)S(1)}, u32[]{:S(2)}, u32[]{:S(2)}) collective-permute-start(bf16[512,256]{1,0:T(8,128)(2,1)S(1)} %get-tuple-element.61), channel_id=1, source_target_pairs={{0,20},{4,16},{8,28},{12,24},{16,4},{20,0},{24,12},{28,8},{1,21},{... | collective-permute-start | bytes 786440 | tf_op jit(solution)/shard_map/ppermute | solution.py:659
  44.0 33.8 %sweeps.1 = (f32[40,128]{1,0:T(8,128)S(1)}, f32[40,128]{1,0:T(8,128)S(1)}, f32[40,128]{1,0:T(8,128)S(1)}, f32[40,128]{1,0:T(8,128)S(1)}, f32[40,128]{1,0:T(8,128...) custom-call(bf16[576,128]{1,0:T(8,128)(2,1)S(1)} %copy-done.1, ...), custom_call_target="tpu_custom_call" | custom-call | flops 42949672960 | bytes 1048576 | tf_op jit(solution)/shard_map/sweeps/pallas_call | solution.py:246
  77.7 8.2 %gather_keys.1.refs_5_ = bf16[8,1024,384]{2,1,0:T(8,128)(2,1)S(1)} custom-call(s32[1]{0:T(128)} %bitcast.index_ref, bf16[576,128]{1,0:T(8,128)(2,1)S(1)} %copy-done.1, bf16[576,128]{1,0:T(8,128)(2,1)S(1)} %collective-permute-done.refs_1_, bf16[576,128]{1,0:T(8,128)(2,1)S(1)} %collective-permute-done.1.refs_2_, ...), custom_call_target="tpu_custom_call" | custom-call | flops 4294967296 | bytes 3145728 | tf_op jit(solution)/shard_map/gather_keys/pallas_call | solution.py:439
  87.0 4.8 %collective-permute-start.10 = (bf16[512,256]{1,0:T(8,128)(2,1)S(1)}, bf16[512,256]{1,0:T(8,128)(2,1)S(1)}, u32[]{:S(2)}, u32[]{:S(2)}) collective-permute-start(bf16[512,256]{1,0:T(8,128)(2,1)S(1)} %get-tuple-element.63), channel_id=1, source_target_pairs={{0,28},{4,24},{8,20},{12,16},{16,12},{20,8},{24,4},{28,0},{1,29},{... | collective-permute-start | bytes 786440 | tf_op jit(solution)/shard_map/ppermute | solution.py:659
  91.8 2.4 %gather_near.1.refs_4_ = bf16[4,1024,256]{2,1,0:T(8,128)(2,1)S(1)} custom-call(s32[1]{0:T(128)} %bitcast.index_ref, bf16[512,256]{1,0:T(8,128)(2,1)S(1)} %get-tuple-element.64.refs_0_, bf16[512,256]{1,0:T(8,128)(2,1)S(1)} %collective-permute-done.11.refs_1_, bf16[512,256]{1,0:T(8,128)(2,1)S(1)} %collective-permute-done.12.refs_2_, ...), custom_call_target="tpu_custom_call" | custom-call | flops 4294967296 | bytes 3145728 | tf_op jit(solution)/shard_map/gather_near/pallas_call | solution.py:452
  94.2 4.7 %collective-permute-done.10.refs_3_ = bf16[512,256]{1,0:T(8,128)(2,1)S(1)} collective-permute-done((bf16[512,256]{1,0:T(8,128)(2,1)S(1)}, bf16[512,256]{1,0:T(8,128)(2,1)S(1)}, u32[]{:S(2)}, u32[]{:S(2)}) %collective-permute-start.10) | collective-permute-done | bytes 262176 | tf_op jit(solution)/shard_map/ppermute | solution.py:659
  99.0 10.9 %attention.1 = (bf16[528,128]{1,0:T(8,128)(2,1)S(1)}, bf16[528,128]{1,0:T(8,128)(2,1)S(1)}, bf16[528,128]{1,0:T(8,128)(2,1)S(1)}, bf16[528,128]{1,0:T(8,128)(2,1...) custom-call(s32[1]{0:T(128)} %bitcast.index_ref, ...), custom_call_target="tpu_custom_call" | custom-call | flops 8589934592 | bytes 4194304 | tf_op jit(solution)/shard_map/attention/pallas_call | solution.py:464
  110.0 8.8 %collective-permute-start.15 = (bf16[528,128]{1,0:T(8,128)(2,1)S(1)}, bf16[528,128]{1,0:T(8,128)(2,1)S(1)}, u32[]{:S(2)}, u32[]{:S(2)}) collective-permute-start(bf16[528,128]{1,0:T(8,128)(2,1)S(1)} %get-tuple-element.44), channel_id=1, source_target_pairs={{0,8},{4,12},{8,0},{12,4},{16,24},{20,28},{24,16},{28,20},{1,9},{5... | collective-permute-start | bytes 405512 | tf_op jit(solution)/shard_map/ppermute | solution.py:659
  118.8 1.4 collective-permute-start.24
  120.2 2.0 %collective-permute-start.16 = (bf16[528,128]{1,0:T(8,128)(2,1)S(1)}, bf16[528,128]{1,0:T(8,128)(2,1)S(1)}, u32[]{:S(2)}, u32[]{:S(2)}) collective-permute-start(bf16[528,128]{1,0:T(8,128)(2,1)S(1)} %get-tuple-element.45), channel_id=1, source_target_pairs={{0,12},{4,8},{8,4},{12,0},{16,28},{20,24},{24,20},{28,16},{1,13},{... | collective-permute-start | bytes 405512 | tf_op jit(solution)/shard_map/ppermute | solution.py:659
  122.5 2.1 %collective-permute-start.17 = (bf16[528,128]{1,0:T(8,128)(2,1)S(1)}, bf16[528,128]{1,0:T(8,128)(2,1)S(1)}, u32[]{:S(2)}, u32[]{:S(2)}) collective-permute-start(bf16[528,128]{1,0:T(8,128)(2,1)S(1)} %get-tuple-element.46), channel_id=1, source_target_pairs={{0,16},{4,20},{8,24},{12,28},{16,0},{20,4},{24,8},{28,12},{1,17},{... | collective-permute-start | bytes 405512 | tf_op jit(solution)/shard_map/ppermute | solution.py:659
  124.6 1.8 %collective-permute-start.18 = (bf16[528,128]{1,0:T(8,128)(2,1)S(1)}, bf16[528,128]{1,0:T(8,128)(2,1)S(1)}, u32[]{:S(2)}, u32[]{:S(2)}) collective-permute-start(bf16[528,128]{1,0:T(8,128)(2,1)S(1)} %get-tuple-element.47), channel_id=1, source_target_pairs={{0,20},{4,16},{8,28},{12,24},{16,4},{20,0},{24,12},{28,8},{1,21},{... | collective-permute-start | bytes 405512 | tf_op jit(solution)/shard_map/ppermute | solution.py:659
  126.4 2.4 %collective-permute-start.19 = (bf16[528,128]{1,0:T(8,128)(2,1)S(1)}, bf16[528,128]{1,0:T(8,128)(2,1)S(1)}, u32[]{:S(2)}, u32[]{:S(2)}) collective-permute-start(bf16[528,128]{1,0:T(8,128)(2,1)S(1)} %get-tuple-element.48), channel_id=1, source_target_pairs={{0,24},{4,28},{8,16},{12,20},{16,8},{20,12},{24,0},{28,4},{1,25},{... | collective-permute-start | bytes 405512 | tf_op jit(solution)/shard_map/ppermute | solution.py:659
  128.7 2.8 %collective-permute-start.20 = (bf16[528,128]{1,0:T(8,128)(2,1)S(1)}, bf16[528,128]{1,0:T(8,128)(2,1)S(1)}, u32[]{:S(2)}, u32[]{:S(2)}) collective-permute-start(bf16[528,128]{1,0:T(8,128)(2,1)S(1)} %get-tuple-element.49), channel_id=1, source_target_pairs={{0,28},{4,24},{8,20},{12,16},{16,12},{20,8},{24,4},{28,0},{1,29},{... | collective-permute-start | bytes 405512 | tf_op jit(solution)/shard_map/ppermute | solution.py:659
  131.6 8.9 %collective-permute-done.17.refs_4_ = bf16[528,128]{1,0:T(8,128)(2,1)S(1)} collective-permute-done((bf16[528,128]{1,0:T(8,128)(2,1)S(1)}, bf16[528,128]{1,0:T(8,128)(2,1)S(1)}, u32[]{:S(2)}, u32[]{:S(2)}) %collective-permute-start.17) | collective-permute-done | bytes 135200 | tf_op jit(solution)/shard_map/ppermute | solution.py:659
  140.5 3.4 %collective-permute-done.18.refs_5_ = bf16[528,128]{1,0:T(8,128)(2,1)S(1)} collective-permute-done((bf16[528,128]{1,0:T(8,128)(2,1)S(1)}, bf16[528,128]{1,0:T(8,128)(2,1)S(1)}, u32[]{:S(2)}, u32[]{:S(2)}) %collective-permute-start.18) | collective-permute-done | bytes 135200 | tf_op jit(solution)/shard_map/ppermute | solution.py:659
  143.9 1.4 collective-permute-start.29
  145.4 2.8 %collective-permute-start.30 = (f32[40,128]{1,0:T(8,128)S(1)}, f32[40,128]{1,0:T(8,128)S(1)}, u32[]{:S(2)}, u32[]{:S(2)}) collective-permute-start(f32[40,128]{1,0:T(8,128)S(1)} %get-tuple-element.56), channel_id=1, source_target_pairs={{0,28},{4,24},{8,20},{12,16},{16,12},{20,8},{24,4},{28,0},{1,29},{... | collective-permute-start | bytes 61448 | tf_op jit(solution)/shard_map/ppermute | solution.py:659
  148.2 1.6 %collective-permute-start.22 = (f32[4,128]{1,0:T(4,128)S(1)}, f32[4,128]{1,0:T(4,128)S(1)}, u32[]{:S(2)}, u32[]{:S(2)}) collective-permute-start(f32[4,128]{1,0:T(4,128)S(1)} %sum_squares.1.refs_8_), channel_id=1, source_target_pairs={{0,2},{1,3},{2,0},{3,1},{4,6},{5,7},{6,4},{7,5},{8,10},{9,11},{10,... | collective-permute-start | bytes 6152 | tf_op jit(solution)/shard_map/ppermute | solution.py:701
  150.0 1.8 %collective-permute-done.30.refs_7_ = f32[40,128]{1,0:T(8,128)S(1)} collective-permute-done((f32[40,128]{1,0:T(8,128)S(1)}, f32[40,128]{1,0:T(8,128)S(1)}, u32[]{:S(2)}, u32[]{:S(2)}) %collective-permute-start.30) | collective-permute-done | bytes 20512 | tf_op jit(solution)/shard_map/ppermute | solution.py:659
  152.9 1.5 norm.1
  (54 shorter events, 5.3 us)
Async XLA Ops:
  3.7 12.7 %collective-permute-start = (bf16[576,128]{1,0:T(8,128)(2,1)}, bf16[576,128]{1,0:T(8,128)(2,1)S(1)}, u32[]{:S(2)}, u32[]{:S(2)}) collective-permute-start(bf16[576,128]{1,0:T(8,128)(2,1)} %get-tuple-element.32), channel_id=1, source_target_pairs={{0,4},{4,0},{8,12},{12,8},{16,20},{20,16},{24,28},{28,24},{1,5},{5... | collective-permute-start | bytes 442376 | tf_op jit(solution)/shard_map/ppermute | solution.py:659
  6.7 13.4 %collective-permute-start.1 = (bf16[576,128]{1,0:T(8,128)(2,1)}, bf16[576,128]{1,0:T(8,128)(2,1)S(1)}, u32[]{:S(2)}, u32[]{:S(2)}) collective-permute-start(bf16[576,128]{1,0:T(8,128)(2,1)} %get-tuple-element.33), channel_id=1, source_target_pairs={{0,8},{4,12},{8,0},{12,4},{16,24},{20,28},{24,16},{28,20},{1,9},{5... | collective-permute-start | bytes 442376 | tf_op jit(solution)/shard_map/ppermute | solution.py:659
  8.2 12.1 %collective-permute-start.2 = (bf16[576,128]{1,0:T(8,128)(2,1)}, bf16[576,128]{1,0:T(8,128)(2,1)S(1)}, u32[]{:S(2)}, u32[]{:S(2)}) collective-permute-start(bf16[576,128]{1,0:T(8,128)(2,1)} %get-tuple-element.34), channel_id=1, source_target_pairs={{0,12},{4,8},{8,4},{12,0},{16,28},{20,24},{24,20},{28,16},{1,13},{... | collective-permute-start | bytes 442376 | tf_op jit(solution)/shard_map/ppermute | solution.py:659
  8.2 12.4 %collective-permute-start.3 = (bf16[576,128]{1,0:T(8,128)(2,1)}, bf16[576,128]{1,0:T(8,128)(2,1)S(1)}, u32[]{:S(2)}, u32[]{:S(2)}) collective-permute-start(bf16[576,128]{1,0:T(8,128)(2,1)} %get-tuple-element.35), channel_id=1, source_target_pairs={{0,16},{4,20},{8,24},{12,28},{16,0},{20,4},{24,8},{28,12},{1,17},{... | collective-permute-start | bytes 442376 | tf_op jit(solution)/shard_map/ppermute | solution.py:659
  11.2 21.8 %collective-permute-start.4 = (bf16[576,128]{1,0:T(8,128)(2,1)}, bf16[576,128]{1,0:T(8,128)(2,1)S(1)}, u32[]{:S(2)}, u32[]{:S(2)}) collective-permute-start(bf16[576,128]{1,0:T(8,128)(2,1)} %get-tuple-element.36), channel_id=1, source_target_pairs={{0,20},{4,16},{8,28},{12,24},{16,4},{20,0},{24,12},{28,8},{1,21},{... | collective-permute-start | bytes 442376 | tf_op jit(solution)/shard_map/ppermute | solution.py:659
  16.4 17.4 %collective-permute-start.5 = (bf16[576,128]{1,0:T(8,128)(2,1)S(1)}, bf16[576,128]{1,0:T(8,128)(2,1)S(1)}, u32[]{:S(2)}, u32[]{:S(2)}) collective-permute-start(bf16[576,128]{1,0:T(8,128)(2,1)S(1)} %copy-done.5), channel_id=1, source_target_pairs={{0,24},{4,28},{8,16},{12,20},{16,8},{20,12},{24,0},{28,4},{1,25},{... | collective-permute-start | bytes 442376 | tf_op jit(solution)/shard_map/ppermute | solution.py:659
  20.1 18.1 %collective-permute-start.6 = (bf16[576,128]{1,0:T(8,128)(2,1)S(1)}, bf16[576,128]{1,0:T(8,128)(2,1)S(1)}, u32[]{:S(2)}, u32[]{:S(2)}) collective-permute-start(bf16[576,128]{1,0:T(8,128)(2,1)S(1)} %copy-done.4), channel_id=1, source_target_pairs={{0,28},{4,24},{8,20},{12,16},{16,12},{20,8},{24,4},{28,0},{1,29},{... | collective-permute-start | bytes 442376 | tf_op jit(solution)/shard_map/ppermute | solution.py:659
  20.3 65.6 %collective-permute-start.12 = (bf16[512,256]{1,0:T(8,128)(2,1)S(1)}, bf16[512,256]{1,0:T(8,128)(2,1)S(1)}, u32[]{:S(2)}, u32[]{:S(2)}) collective-permute-start(bf16[512,256]{1,0:T(8,128)(2,1)S(1)} %get-tuple-element.65), channel_id=1, source_target_pairs={{0,8},{4,12},{8,0},{12,4},{16,24},{20,28},{24,16},{28,20},{1,9},{5... | collective-permute-start | bytes 786440 | tf_op jit(solution)/shard_map/ppermute | solution.py:659
  20.7 66.3 %collective-permute-start.11 = (bf16[512,256]{1,0:T(8,128)(2,1)S(1)}, bf16[512,256]{1,0:T(8,128)(2,1)S(1)}, u32[]{:S(2)}, u32[]{:S(2)}) collective-permute-start(bf16[512,256]{1,0:T(8,128)(2,1)S(1)} %get-tuple-element.66), channel_id=1, source_target_pairs={{0,4},{4,0},{8,12},{12,8},{16,20},{20,16},{24,28},{28,24},{1,5},{5... | collective-permute-start | bytes 786440 | tf_op jit(solution)/shard_map/ppermute | solution.py:659
  33.0 58.8 %collective-permute-start.13 = (bf16[512,256]{1,0:T(8,128)(2,1)S(1)}, bf16[512,256]{1,0:T(8,128)(2,1)S(1)}, u32[]{:S(2)}, u32[]{:S(2)}) collective-permute-start(bf16[512,256]{1,0:T(8,128)(2,1)S(1)} %get-tuple-element.59), channel_id=1, source_target_pairs={{0,12},{4,8},{8,4},{12,0},{16,28},{20,24},{24,20},{28,16},{1,13},{... | collective-permute-start | bytes 786440 | tf_op jit(solution)/shard_map/ppermute | solution.py:659
  33.9 60.4 %collective-permute-start.7 = (bf16[512,256]{1,0:T(8,128)(2,1)S(1)}, bf16[512,256]{1,0:T(8,128)(2,1)S(1)}, u32[]{:S(2)}, u32[]{:S(2)}) collective-permute-start(bf16[512,256]{1,0:T(8,128)(2,1)S(1)} %get-tuple-element.60), channel_id=1, source_target_pairs={{0,16},{4,20},{8,24},{12,28},{16,0},{20,4},{24,8},{28,12},{1,17},{... | collective-permute-start | bytes 786440 | tf_op jit(solution)/shard_map/ppermute | solution.py:659
  38.2 56.0 %collective-permute-start.8 = (bf16[512,256]{1,0:T(8,128)(2,1)S(1)}, bf16[512,256]{1,0:T(8,128)(2,1)S(1)}, u32[]{:S(2)}, u32[]{:S(2)}) collective-permute-start(bf16[512,256]{1,0:T(8,128)(2,1)S(1)} %get-tuple-element.61), channel_id=1, source_target_pairs={{0,20},{4,16},{8,28},{12,24},{16,4},{20,0},{24,12},{28,8},{1,21},{... | collective-permute-start | bytes 786440 | tf_op jit(solution)/shard_map/ppermute | solution.py:659
  86.0 8.3 %collective-permute-start.9 = (bf16[512,256]{1,0:T(8,128)(2,1)S(1)}, bf16[512,256]{1,0:T(8,128)(2,1)S(1)}, u32[]{:S(2)}, u32[]{:S(2)}) collective-permute-start(bf16[512,256]{1,0:T(8,128)(2,1)S(1)} %get-tuple-element.62), channel_id=1, source_target_pairs={{0,24},{4,28},{8,16},{12,20},{16,8},{20,12},{24,0},{28,4},{1,25},{... | collective-permute-start | bytes 786440 | tf_op jit(solution)/shard_map/ppermute | solution.py:659
  87.0 11.9 %collective-permute-start.10 = (bf16[512,256]{1,0:T(8,128)(2,1)S(1)}, bf16[512,256]{1,0:T(8,128)(2,1)S(1)}, u32[]{:S(2)}, u32[]{:S(2)}) collective-permute-start(bf16[512,256]{1,0:T(8,128)(2,1)S(1)} %get-tuple-element.63), channel_id=1, source_target_pairs={{0,28},{4,24},{8,20},{12,16},{16,12},{20,8},{24,4},{28,0},{1,29},{... | collective-permute-start | bytes 786440 | tf_op jit(solution)/shard_map/ppermute | solution.py:659
  99.0 53.9 %copy-start.2 = (f32[1024]{0:T(1024)S(1)}, f32[1024]{0:T(1024)}, u32[]{:S(2)}) copy-start(f32[1024]{0:T(1024)} %param.11) | copy-start | bytes 12292
  109.9 16.5 %collective-permute-start.14 = (bf16[528,128]{1,0:T(8,128)(2,1)S(1)}, bf16[528,128]{1,0:T(8,128)(2,1)S(1)}, u32[]{:S(2)}, u32[]{:S(2)}) collective-permute-start(bf16[528,128]{1,0:T(8,128)(2,1)S(1)} %get-tuple-element.43), channel_id=1, source_target_pairs={{0,4},{4,0},{8,12},{12,8},{16,20},{20,16},{24,28},{28,24},{1,5},{5... | collective-permute-start | bytes 405512 | tf_op jit(solution)/shard_map/ppermute | solution.py:659
  110.0 18.8 %collective-permute-start.15 = (bf16[528,128]{1,0:T(8,128)(2,1)S(1)}, bf16[528,128]{1,0:T(8,128)(2,1)S(1)}, u32[]{:S(2)}, u32[]{:S(2)}) collective-permute-start(bf16[528,128]{1,0:T(8,128)(2,1)S(1)} %get-tuple-element.44), channel_id=1, source_target_pairs={{0,8},{4,12},{8,0},{12,4},{16,24},{20,28},{24,16},{28,20},{1,9},{5... | collective-permute-start | bytes 405512 | tf_op jit(solution)/shard_map/ppermute | solution.py:659
  118.8 3.8 %collective-permute-start.24 = (f32[40,128]{1,0:T(8,128)S(1)}, f32[40,128]{1,0:T(8,128)S(1)}, u32[]{:S(2)}, u32[]{:S(2)}) collective-permute-start(f32[40,128]{1,0:T(8,128)S(1)} %get-tuple-element.50), channel_id=1, source_target_pairs={{0,4},{4,0},{8,12},{12,8},{16,20},{20,16},{24,28},{28,24},{1,5},{5... | collective-permute-start | bytes 61448 | tf_op jit(solution)/shard_map/ppermute | solution.py:659
  120.2 4.4 %collective-permute-start.25 = (f32[40,128]{1,0:T(8,128)S(1)}, f32[40,128]{1,0:T(8,128)S(1)}, u32[]{:S(2)}, u32[]{:S(2)}) collective-permute-start(f32[40,128]{1,0:T(8,128)S(1)} %get-tuple-element.51), channel_id=1, source_target_pairs={{0,8},{4,12},{8,0},{12,4},{16,24},{20,28},{24,16},{28,20},{1,9},{5... | collective-permute-start | bytes 61448 | tf_op jit(solution)/shard_map/ppermute | solution.py:659
  120.2 11.4 %collective-permute-start.16 = (bf16[528,128]{1,0:T(8,128)(2,1)S(1)}, bf16[528,128]{1,0:T(8,128)(2,1)S(1)}, u32[]{:S(2)}, u32[]{:S(2)}) collective-permute-start(bf16[528,128]{1,0:T(8,128)(2,1)S(1)} %get-tuple-element.45), channel_id=1, source_target_pairs={{0,12},{4,8},{8,4},{12,0},{16,28},{20,24},{24,20},{28,16},{1,13},{... | collective-permute-start | bytes 405512 | tf_op jit(solution)/shard_map/ppermute | solution.py:659
  122.5 17.9 %collective-permute-start.17 = (bf16[528,128]{1,0:T(8,128)(2,1)S(1)}, bf16[528,128]{1,0:T(8,128)(2,1)S(1)}, u32[]{:S(2)}, u32[]{:S(2)}) collective-permute-start(bf16[528,128]{1,0:T(8,128)(2,1)S(1)} %get-tuple-element.46), channel_id=1, source_target_pairs={{0,16},{4,20},{8,24},{12,28},{16,0},{20,4},{24,8},{28,12},{1,17},{... | collective-permute-start | bytes 405512 | tf_op jit(solution)/shard_map/ppermute | solution.py:659
  124.6 19.3 %collective-permute-start.18 = (bf16[528,128]{1,0:T(8,128)(2,1)S(1)}, bf16[528,128]{1,0:T(8,128)(2,1)S(1)}, u32[]{:S(2)}, u32[]{:S(2)}) collective-permute-start(bf16[528,128]{1,0:T(8,128)(2,1)S(1)} %get-tuple-element.47), channel_id=1, source_target_pairs={{0,20},{4,16},{8,28},{12,24},{16,4},{20,0},{24,12},{28,8},{1,21},{... | collective-permute-start | bytes 405512 | tf_op jit(solution)/shard_map/ppermute | solution.py:659
  126.4 17.5 %collective-permute-start.19 = (bf16[528,128]{1,0:T(8,128)(2,1)S(1)}, bf16[528,128]{1,0:T(8,128)(2,1)S(1)}, u32[]{:S(2)}, u32[]{:S(2)}) collective-permute-start(bf16[528,128]{1,0:T(8,128)(2,1)S(1)} %get-tuple-element.48), channel_id=1, source_target_pairs={{0,24},{4,28},{8,16},{12,20},{16,8},{20,12},{24,0},{28,4},{1,25},{... | collective-permute-start | bytes 405512 | tf_op jit(solution)/shard_map/ppermute | solution.py:659
  128.7 16.6 %collective-permute-start.20 = (bf16[528,128]{1,0:T(8,128)(2,1)S(1)}, bf16[528,128]{1,0:T(8,128)(2,1)S(1)}, u32[]{:S(2)}, u32[]{:S(2)}) collective-permute-start(bf16[528,128]{1,0:T(8,128)(2,1)S(1)} %get-tuple-element.49), channel_id=1, source_target_pairs={{0,28},{4,24},{8,20},{12,16},{16,12},{20,8},{24,4},{28,0},{1,29},{... | collective-permute-start | bytes 405512 | tf_op jit(solution)/shard_map/ppermute | solution.py:659
  131.6 16.6 %collective-permute-start.26 = (f32[40,128]{1,0:T(8,128)S(1)}, f32[40,128]{1,0:T(8,128)S(1)}, u32[]{:S(2)}, u32[]{:S(2)}) collective-permute-start(f32[40,128]{1,0:T(8,128)S(1)} %get-tuple-element.52), channel_id=1, source_target_pairs={{0,12},{4,8},{8,4},{12,0},{16,28},{20,24},{24,20},{28,16},{1,13},{... | collective-permute-start | bytes 61448 | tf_op jit(solution)/shard_map/ppermute | solution.py:659
  140.5 7.8 %collective-permute-start.27 = (f32[40,128]{1,0:T(8,128)S(1)}, f32[40,128]{1,0:T(8,128)S(1)}, u32[]{:S(2)}, u32[]{:S(2)}) collective-permute-start(f32[40,128]{1,0:T(8,128)S(1)} %get-tuple-element.53), channel_id=1, source_target_pairs={{0,16},{4,20},{8,24},{12,28},{16,0},{20,4},{24,8},{28,12},{1,17},{... | collective-permute-start | bytes 61448 | tf_op jit(solution)/shard_map/ppermute | solution.py:659
  143.9 6.0 %collective-permute-start.28 = (f32[40,128]{1,0:T(8,128)S(1)}, f32[40,128]{1,0:T(8,128)S(1)}, u32[]{:S(2)}, u32[]{:S(2)}) collective-permute-start(f32[40,128]{1,0:T(8,128)S(1)} %get-tuple-element.54), channel_id=1, source_target_pairs={{0,20},{4,16},{8,28},{12,24},{16,4},{20,0},{24,12},{28,8},{1,21},{... | collective-permute-start | bytes 61448 | tf_op jit(solution)/shard_map/ppermute | solution.py:659
  143.9 6.1 %collective-permute-start.29 = (f32[40,128]{1,0:T(8,128)S(1)}, f32[40,128]{1,0:T(8,128)S(1)}, u32[]{:S(2)}, u32[]{:S(2)}) collective-permute-start(f32[40,128]{1,0:T(8,128)S(1)} %get-tuple-element.55), channel_id=1, source_target_pairs={{0,24},{4,28},{8,16},{12,20},{16,8},{20,12},{24,0},{28,4},{1,25},{... | collective-permute-start | bytes 61448 | tf_op jit(solution)/shard_map/ppermute | solution.py:659
  145.4 6.5 %collective-permute-start.30 = (f32[40,128]{1,0:T(8,128)S(1)}, f32[40,128]{1,0:T(8,128)S(1)}, u32[]{:S(2)}, u32[]{:S(2)}) collective-permute-start(f32[40,128]{1,0:T(8,128)S(1)} %get-tuple-element.56), channel_id=1, source_target_pairs={{0,28},{4,24},{8,20},{12,16},{16,12},{20,8},{24,4},{28,0},{1,29},{... | collective-permute-start | bytes 61448 | tf_op jit(solution)/shard_map/ppermute | solution.py:659
  148.2 4.4 %collective-permute-start.23 = (f32[4,128]{1,0:T(4,128)S(1)}, f32[4,128]{1,0:T(4,128)S(1)}, u32[]{:S(2)}, u32[]{:S(2)}) collective-permute-start(f32[4,128]{1,0:T(4,128)S(1)} %sum_squares.1.refs_8_), channel_id=1, source_target_pairs={{0,3},{1,0},{2,1},{3,2},{4,7},{5,4},{6,5},{7,6},{8,11},{9,8},{10,9... | collective-permute-start | bytes 6152 | tf_op jit(solution)/shard_map/ppermute | solution.py:701
  148.2 4.3 %collective-permute-start.22 = (f32[4,128]{1,0:T(4,128)S(1)}, f32[4,128]{1,0:T(4,128)S(1)}, u32[]{:S(2)}, u32[]{:S(2)}) collective-permute-start(f32[4,128]{1,0:T(4,128)S(1)} %sum_squares.1.refs_8_), channel_id=1, source_target_pairs={{0,2},{1,3},{2,0},{3,1},{4,6},{5,7},{6,4},{7,5},{8,10},{9,11},{10,... | collective-permute-start | bytes 6152 | tf_op jit(solution)/shard_map/ppermute | solution.py:701
  149.9 3.0 %collective-permute-start.21 = (f32[4,128]{1,0:T(4,128)S(1)}, f32[4,128]{1,0:T(4,128)S(1)}, u32[]{:S(2)}, u32[]{:S(2)}) collective-permute-start(f32[4,128]{1,0:T(4,128)S(1)} %sum_squares.1.refs_8_), channel_id=1, source_target_pairs={{0,1},{1,2},{2,3},{3,0},{4,5},{5,6},{6,7},{7,4},{8,9},{9,10},{10,1... | collective-permute-start | bytes 6152 | tf_op jit(solution)/shard_map/ppermute | solution.py:701
  (5 other events, 49.2 us)
